TPU v7x, 32 devices: a whole 2x2x4 slice. The times are simulated.
32 devices in a mesh: fsdp: 8 (over y, x, core), seq: 4 (over z).
Axes of the slice: x: 2, y: 2, z: 4, core: 2. Of those that a mesh axis runs over, the one named last changes fastest.
Arguments:
- latents_in: bfloat16 [2, 8, 128, 768], P(None, 'fsdp'), may hold values from -6 to 6
- inputs: bfloat16 [2, 8, 6312, 768], P(None, 'fsdp', 'seq'), may hold values from -6 to 6
- clip_frames: int32 [2, 8], P(None, 'fsdp'), may hold values from 4 to 16
- text_mask: int32 [2, 8, 40], P(None, 'fsdp'), may hold values 0 or 1
- qkv_weight: bfloat16 [2, 3, 768, 768], P(None, None, 'fsdp'), may hold values from -0.21875 to 0.21875
- out_weight: bfloat16 [2, 768, 768], P(None, 'fsdp'), may hold values from -1.75 to 1.75
- mlp_in: bfloat16 [2, 768, 3072], P(None, 'fsdp'), may hold values from -0.21875 to 0.21875
- mlp_out: bfloat16 [2, 3072, 768], P(None, 'fsdp'), may hold values from -0.109375 to 0.109375
- norm_gain: bfloat16 [5, 768], P(None, 'fsdp'), may hold values from 0.5 to 1.5
- norm_bias: bfloat16 [5, 768], P(None, 'fsdp'), may hold values from -2.5 to 2.5
- bias_in: bfloat16 [2, 3072], P(None, 'fsdp'), may hold values from -2.5 to 2.5
- bias_out: bfloat16 [2, 768], P(None, 'fsdp'), may hold values from -2.5 to 2.5
- out_cotangent: bfloat16 [2, 8, 128, 768], P(None, 'fsdp'), may hold values from -6 to 6
Outputs:
- latents_out: float32 [2, 8, 128, 768], P(None, 'fsdp')
- latents_grad: float32 [2, 8, 128, 768], P(None, 'fsdp')
- inputs_grad: float32 [2, 8, 6312, 768], P(None, 'fsdp', 'seq')
- qkv_grad: float32 [2, 3, 768, 768], P(None, None, 'fsdp')
- out_weight_grad: float32 [2, 768, 768], P(None, 'fsdp')
- mlp_in_grad: float32 [2, 768, 3072], P(None, 'fsdp')
- mlp_out_grad: float32 [2, 3072, 768], P(None, 'fsdp')
- norm_gain_grad: float32 [5, 768], P(None, 'fsdp')
- norm_bias_grad: float32 [5, 768], P(None, 'fsdp')
- bias_in_grad: float32 [2, 3072], P(None, 'fsdp')
- bias_out_grad: float32 [2, 768], P(None, 'fsdp')
Inputs may be any that keep to these rules, and one draw needn't show every extreme that they name: `clip_frames`: frames of each clip; its first 392 times that many patch slots hold tokens, the rest of its 16 frame slots are padding.
All inputs are finite; a program needn't handle non-finite values. No bound on the sum of `text_mask` on one device may be relied on, other than what follows from the above.
Results may differ from a plain program's by a relative error of at most 0.015.
Values may be sent and summed in bfloat16 or wider, within the bound.
No kernel may reach another device: no remote copies, remote signals or barrier semaphores. Data moves between devices by JAX's collectives and lax.ppermute only.
A program may use at most 320 MiB of HBM per device.

v0:
```python
import jax
import jax.numpy as jnp
from jax import lax
from jax.sharding import PartitionSpec as P

D = 768
HEADS = 12
HEAD = 64
PATCHES = 392
FRAMES = 16


epsilon = 1e-06


def layer_norm(values, scales, offsets):
    center = values - jnp.mean(values, -1, keepdims=True)
    spread = jnp.mean(center * center, -1, keepdims=True)
    return center * lax.rsqrt(spread + epsilon) * scales + offsets


def to_half(values):
    return values.astype(jnp.bfloat16)


def product(form, left, right):
    return jnp.einsum(form, left, right, preferred_element_type=jnp.float32)


def norm_back(values, scales, offsets, grad_normed):
    unused, pullback = jax.vjp(layer_norm, values, scales, offsets)
    return pullback(grad_normed)


def feed_forward(residual, up_w, down_w, up_b, down_b, scales, offsets):
    normed = to_half(layer_norm(residual, scales, offsets))
    hidden = product("cnd,df->cnf", normed, up_w) + up_b
    active = to_half(jax.nn.gelu(hidden))
    result = product("cnf,fd->cnd", active, down_w) + down_b
    return (result, (residual, normed, hidden, active))


def feed_back(stored, grad_in, up_w, down_w, scales, offsets):
    residual, normed, hidden, active = stored
    grad_y = to_half(grad_in)
    grad_down = product("cnf,cnd->fd", active, grad_y)
    grad_down_b = jnp.sum(grad_y, (0, 1), dtype=jnp.float32)
    grad_act = product("cnd,fd->cnf", grad_y, down_w)
    unused, gelu_pull = jax.vjp(jax.nn.gelu, hidden)
    grad_hidden = to_half(gelu_pull(grad_act)[0])
    grad_up = product("cnd,cnf->df", normed, grad_hidden)
    grad_up_b = jnp.sum(grad_hidden, (0, 1), dtype=jnp.float32)
    grad_normed = product("cnf,df->cnd", grad_hidden, up_w)
    grad_rows, grad_scales, grad_offsets = norm_back(residual, scales, offsets, grad_normed)
    return (grad_rows, (grad_up, grad_down, grad_up_b, grad_down_b, grad_scales, grad_offsets))


def self_forward(residual, qkv_w, out_w, scales, offsets):
    clip_count, latent_count = (residual.shape[0], residual.shape[1])
    normed = to_half(layer_norm(residual, scales, offsets))
    heads_qkv = to_half(product("cnd,jde->jcne", normed, qkv_w)).reshape(
        3, clip_count, latent_count, HEADS, HEAD
    )
    scores = product("cqhd,ckhd->cqhk", heads_qkv[0], heads_qkv[1]) * 0.125
    row_peak = jnp.max(scores, -1, keepdims=True)
    self_exp = jnp.exp(scores - row_peak)
    softmax_w = self_exp / jnp.sum(self_exp, -1, keepdims=True)
    mixed_heads = to_half(product("cqhk,ckhd->cqhd", to_half(softmax_w), heads_qkv[2])).reshape(
        clip_count, latent_count, D
    )
    result = product("cnd,de->cne", mixed_heads, out_w)
    return (result, (residual, normed, heads_qkv, softmax_w, mixed_heads))


def self_back(stored, grad_in, qkv_w, out_w, scales, offsets):
    residual, normed, heads_qkv, softmax_w, mixed_heads = stored
    clip_count, latent_count = (residual.shape[0], residual.shape[1])
    grad_a = to_half(grad_in)
    grad_out_w = product("cnd,cne->de", mixed_heads, grad_a)
    grad_mixed = to_half(product("cne,de->cnd", grad_a, out_w)).reshape(
        clip_count, latent_count, HEADS, HEAD
    )
    grad_probs = product("cqhd,ckhd->cqhk", grad_mixed, heads_qkv[2])
    grad_values = to_half(product("cqhk,cqhd->ckhd", to_half(softmax_w), grad_mixed))
    grad_scores = to_half(
        softmax_w * (grad_probs - jnp.sum(softmax_w * grad_probs, -1, keepdims=True))
    )
    grad_queries = to_half(product("cqhk,ckhd->cqhd", grad_scores, heads_qkv[1]) * 0.125)
    grad_keys = to_half(product("cqhk,cqhd->ckhd", grad_scores, heads_qkv[0]) * 0.125)
    stacked = jnp.stack([grad_queries, grad_keys, grad_values]).reshape(
        3, clip_count, latent_count, D
    )
    grad_qkv = product("cnd,jcne->jde", normed, stacked)
    grad_normed = product("jcne,jde->cnd", stacked, qkv_w)
    grad_rows, grad_scales, grad_offsets = norm_back(residual, scales, offsets, grad_normed)
    return (grad_rows, (grad_qkv, grad_out_w, grad_scales, grad_offsets))


def cross_scores(queries, key_heads, valid_keys):
    scores = product("cqhd,ckhd->cqhk", queries, key_heads) * 0.125
    return jnp.where(valid_keys[:, None, None, :], jnp.exp(scores), 0.0)


def cross_forward(residual, tokens, valid_keys, qkv_w, out_w, scales, offsets):
    clip_count, latent_count, local_len = (residual.shape[0], residual.shape[1], tokens.shape[1])
    latent_normed = to_half(layer_norm(residual, scales[0], offsets[0]))
    token_normed = to_half(layer_norm(tokens, scales[1], offsets[1]))
    queries = to_half(product("cnd,de->cne", latent_normed, qkv_w[0])).reshape(
        clip_count, latent_count, HEADS, HEAD
    )
    keyval = to_half(product("cld,jde->jcle", token_normed, qkv_w[1:3])).reshape(
        2, clip_count, local_len, HEADS, HEAD
    )
    weights_exp = cross_scores(queries, keyval[0], valid_keys)
    numer_part = product("cqhk,ckhd->cqhd", to_half(weights_exp), keyval[1])
    numer_share, total_share = (
        lax.psum_scatter(numer_part, "seq", scatter_dimension=2, tiled=True),
        lax.psum_scatter(jnp.sum(weights_exp, -1), "seq", scatter_dimension=2, tiled=True),
    )
    numerator, totals = (
        lax.all_gather(numer_share, "seq", axis=2, tiled=True),
        lax.all_gather(total_share, "seq", axis=2, tiled=True),
    )
    attended = to_half(numerator / totals[..., None]).reshape(clip_count, latent_count, D)
    result = product("cnd,de->cne", attended, out_w)
    return (
        result,
        (
            residual,
            tokens,
            latent_normed,
            token_normed,
            queries,
            keyval,
            numerator,
            totals,
            attended,
        ),
    )


def cross_back(stored, grad_in, valid_keys, qkv_w, out_w, scales, offsets):
    residual, tokens, latent_normed, token_normed, queries, keyval, numerator, totals, attended = (
        stored
    )
    clip_count, latent_count, local_len = (residual.shape[0], residual.shape[1], tokens.shape[1])
    grad_a = to_half(grad_in)
    grad_out_w = product("cnd,cne->de", attended, grad_a)
    grad_att = (
        to_half(product("cne,de->cnd", grad_a, out_w))
        .reshape(clip_count, latent_count, HEADS, HEAD)
        .astype(jnp.float32)
    )
    grad_numer = to_half(grad_att / totals[..., None])
    grad_totals = -jnp.sum(grad_att * numerator, -1) / (totals * totals)
    weights_exp = cross_scores(queries, keyval[0], valid_keys)
    grad_weights = product("cqhd,ckhd->cqhk", grad_numer, keyval[1]) + grad_totals[..., None]
    grad_scores = to_half(weights_exp * grad_weights)
    grad_values = to_half(product("cqhk,cqhd->ckhd", to_half(weights_exp), grad_numer))
    grad_keys = to_half(product("cqhk,cqhd->ckhd", grad_scores, queries) * 0.125)
    grad_query_part = product("cqhk,ckhd->cqhd", grad_scores, keyval[0]) * 0.125
    query_share = lax.psum_scatter(
        grad_query_part.astype(jnp.bfloat16), "seq", scatter_dimension=2, tiled=True
    ).astype(jnp.float32)
    grad_queries = lax.all_gather(to_half(query_share), "seq", axis=2, tiled=True).reshape(
        clip_count, latent_count, D
    )
    grad_kv = jnp.stack([grad_keys, grad_values]).reshape(2, clip_count, local_len, D)
    grad_q_w = product("cnd,cne->de", latent_normed, grad_queries)
    grad_kv_w = product("cld,jcle->jde", token_normed, grad_kv)
    grad_latent_norm = product("cne,de->cnd", grad_queries, qkv_w[0])
    grad_token_norm = product("jcle,jde->cld", grad_kv, qkv_w[1:3])
    grad_rows, grad_scale_lat, grad_shift_lat = norm_back(
        residual, scales[0], offsets[0], grad_latent_norm
    )
    grad_tokens, grad_scale_tok, grad_shift_tok = norm_back(
        tokens, scales[1], offsets[1], grad_token_norm
    )
    grad_qkv = jnp.concatenate([grad_q_w[None], grad_kv_w])
    return (
        grad_rows,
        grad_tokens,
        (
            grad_qkv,
            grad_out_w,
            jnp.stack([grad_scale_lat, grad_scale_tok]),
            jnp.stack([grad_shift_lat, grad_shift_tok]),
        ),
    )


def per_device(
    latents_in,
    inputs,
    clip_frames,
    text_mask,
    qkv_weight,
    out_weight,
    mlp_in,
    mlp_out,
    norm_gain,
    norm_bias,
    bias_in,
    bias_out,
    out_cotangent,
):
    local_len = inputs.shape[2]
    seq_start = lax.axis_index("seq") * local_len
    positions = jnp.arange(FRAMES * PATCHES, dtype=jnp.int32)
    grad_sum = None
    finals = []
    latent_grads = []
    token_grads = []
    for micro_step in range(latents_in.shape[0]):
        gathered = (
            lax.all_gather(qkv_weight, "fsdp", axis=2, tiled=True),
            lax.all_gather(out_weight, "fsdp", axis=1, tiled=True),
            lax.all_gather(mlp_in, "fsdp", axis=1, tiled=True),
            lax.all_gather(mlp_out, "fsdp", axis=1, tiled=True),
            lax.all_gather(norm_gain, "fsdp", axis=1, tiled=True),
            lax.all_gather(norm_bias, "fsdp", axis=1, tiled=True),
            lax.all_gather(bias_in, "fsdp", axis=1, tiled=True),
            lax.all_gather(bias_out, "fsdp", axis=1, tiled=True),
        )
        qkv_w, out_w, up_w, down_w, gain_w, shift_w, up_bias, down_bias = gathered
        scales = gain_w.astype(jnp.float32)
        offsets = shift_w.astype(jnp.float32)
        up_b32 = up_bias.astype(jnp.float32)
        down_b32 = down_bias.astype(jnp.float32)
        frames_now = clip_frames[micro_step]
        full_mask = jnp.concatenate(
            [positions[None, :] < frames_now[:, None] * PATCHES, text_mask[micro_step] > 0], axis=1
        )
        valid_keys = lax.dynamic_slice_in_dim(full_mask, seq_start, local_len, 1)
        start_rows = latents_in[micro_step].astype(jnp.float32)
        token_rows = inputs[micro_step].astype(jnp.float32)
        cross_out, cross_saved = cross_forward(
            start_rows, token_rows, valid_keys, qkv_w[0], out_w[0], scales, offsets
        )
        first = start_rows + cross_out
        ff_one, ff_one_saved = feed_forward(
            first, up_w[0], down_w[0], up_b32[0], down_b32[0], scales[2], offsets[2]
        )
        second = first + ff_one
        self_out, self_saved = self_forward(second, qkv_w[1], out_w[1], scales[3], offsets[3])
        third = second + self_out
        ff_two, ff_two_saved = feed_forward(
            third, up_w[1], down_w[1], up_b32[1], down_b32[1], scales[4], offsets[4]
        )
        finals.append(third + ff_two)
        gathered = (
            lax.all_gather(qkv_weight, "fsdp", axis=2, tiled=True),
            lax.all_gather(out_weight, "fsdp", axis=1, tiled=True),
            lax.all_gather(mlp_in, "fsdp", axis=1, tiled=True),
            lax.all_gather(mlp_out, "fsdp", axis=1, tiled=True),
            lax.all_gather(norm_gain, "fsdp", axis=1, tiled=True),
            lax.all_gather(norm_bias, "fsdp", axis=1, tiled=True),
            lax.all_gather(bias_in, "fsdp", axis=1, tiled=True),
            lax.all_gather(bias_out, "fsdp", axis=1, tiled=True),
        )
        qkv_w, out_w, up_w, down_w, gain_w, shift_w, up_bias, down_bias = gathered
        scales = gain_w.astype(jnp.float32)
        offsets = shift_w.astype(jnp.float32)
        grad_four = out_cotangent[micro_step].astype(jnp.float32)
        grad_three, ff_two_grads = feed_back(
            ff_two_saved, grad_four, up_w[1], down_w[1], scales[4], offsets[4]
        )
        grad_three = grad_three + grad_four
        grad_two, self_grads = self_back(
            self_saved, grad_three, qkv_w[1], out_w[1], scales[3], offsets[3]
        )
        grad_two = grad_two + grad_three
        grad_one, ff_one_grads = feed_back(
            ff_one_saved, grad_two, up_w[0], down_w[0], scales[2], offsets[2]
        )
        grad_one = grad_one + grad_two
        grad_start, grad_tokens, cross_grads = cross_back(
            cross_saved, grad_one, valid_keys, qkv_w[0], out_w[0], scales, offsets
        )
        latent_grads.append(grad_start + grad_one)
        token_grads.append(grad_tokens)
        grad_qkv_all = jnp.stack([cross_grads[0], self_grads[0]])
        grad_out_all = jnp.stack([cross_grads[1], self_grads[1]])
        grad_up_all = jnp.stack([ff_one_grads[0], ff_two_grads[0]])
        grad_down_all = jnp.stack([ff_one_grads[1], ff_two_grads[1]])
        grad_gain_all = jnp.concatenate(
            [cross_grads[2], jnp.stack([ff_one_grads[4], self_grads[2], ff_two_grads[4]])]
        )
        grad_shift_all = jnp.concatenate(
            [cross_grads[3], jnp.stack([ff_one_grads[5], self_grads[3], ff_two_grads[5]])]
        )
        grad_upb_all = jnp.stack([ff_one_grads[2], ff_two_grads[2]])
        grad_downb_all = jnp.stack([ff_one_grads[3], ff_two_grads[3]])
        grad_step = (
            grad_qkv_all,
            grad_out_all,
            grad_up_all,
            grad_down_all,
            grad_gain_all,
            grad_shift_all,
            grad_upb_all,
            grad_downb_all,
        )
        grad_sum = grad_step if grad_sum is None else jax.tree.map(jnp.add, grad_sum, grad_step)
    grad_sum = (
        lax.psum_scatter(grad_sum[0], "fsdp", scatter_dimension=2, tiled=True),
        lax.psum_scatter(grad_sum[1], "fsdp", scatter_dimension=1, tiled=True),
        lax.psum_scatter(grad_sum[2], "fsdp", scatter_dimension=1, tiled=True),
        lax.psum_scatter(grad_sum[3], "fsdp", scatter_dimension=1, tiled=True),
        lax.psum_scatter(grad_sum[4], "fsdp", scatter_dimension=1, tiled=True),
        lax.psum_scatter(grad_sum[5], "fsdp", scatter_dimension=1, tiled=True),
        lax.psum_scatter(grad_sum[6], "fsdp", scatter_dimension=1, tiled=True),
        lax.psum_scatter(grad_sum[7], "fsdp", scatter_dimension=1, tiled=True),
    )
    kv_part, gain_part, shift_part = (
        lax.psum(grad_sum[0][0, 1:3].astype(jnp.bfloat16), "seq").astype(jnp.float32),
        lax.psum(grad_sum[4][1].astype(jnp.bfloat16), "seq").astype(jnp.float32),
        lax.psum(grad_sum[5][1].astype(jnp.bfloat16), "seq").astype(jnp.float32),
    )
    qkv_final = grad_sum[0].at[0, 1:3].set(kv_part)
    gain_final = grad_sum[4].at[1].set(gain_part)
    shift_final = grad_sum[5].at[1].set(shift_part)
    return (
        jnp.stack(finals),
        jnp.stack(latent_grads),
        jnp.stack(token_grads),
        qkv_final,
        grad_sum[1],
        grad_sum[2],
        grad_sum[3],
        gain_final,
        shift_final,
        grad_sum[6],
        grad_sum[7],
    )


def solution(mesh):
    in_specs = (
        P(None, "fsdp", None, None),
        P(None, "fsdp", "seq", None),
        P(None, "fsdp"),
        P(None, "fsdp", None),
        P(None, None, "fsdp", None),
        P(None, "fsdp", None),
        P(None, "fsdp", None),
        P(None, "fsdp", None),
        P(None, "fsdp"),
        P(None, "fsdp"),
        P(None, "fsdp"),
        P(None, "fsdp"),
        P(None, "fsdp", None, None),
    )
    out_specs = (
        P(None, "fsdp", None, None),
        P(None, "fsdp", None, None),
        P(None, "fsdp", "seq", None),
        P(None, None, "fsdp", None),
        P(None, "fsdp", None),
        P(None, "fsdp", None),
        P(None, "fsdp", None),
        P(None, "fsdp"),
        P(None, "fsdp"),
        P(None, "fsdp"),
        P(None, "fsdp"),
    )
    return jax.shard_map(
        per_device, mesh=mesh, in_specs=in_specs, out_specs=out_specs, check_vma=False
    )
```

profile of v0, /device:TPU:0, one launch (start us, length us, event | category | flops | bytes accessed | tf_op | source)
XLA Modules:
  0.0 1272.3 jit_solution(13977146467657318002)
XLA Ops:
  8.0 10.5 all-gather.1
  18.5 8.8 all-gather
  32.8 10.1 fusion.290
  46.0 15.5 %all-gather.8.cloned.1.call-done = bf16[2,3,768,768]{3,2,1,0:T(8,128)(2,1)} async-done(((bf16[2,3,96,768]{3,2,1,0:T(8,128)(2,1)}), bf16[2,3,768,768]{3,2,1,0:T(8,128)(2,1)}) %all-gather.8.cloned.1.call-update) | async-done | bytes 7077904 | tf_op jit(solution)/shard_map/all_gather | solution.py:216
  61.6 6.4 convert_bitcast_fusion.4
  81.3 5.0 bitcast_reduce_fusion
  97.5 6.7 convert_bitcast_fusion.5
  117.6 5.0 bitcast_reduce_fusion.1
  130.3 8.7 all-gather.2
  140.4 8.0 all_gather.67
  149.6 18.7 %all-reduce.3 = (f32[1,128,12]{1,0,2:T(1,128)S(1)}, f32[1,128,12]{1,0,2:T(1,128)S(1)}) all-reduce(f32[1,128,12]{1,0,2:T(1,128)S(1)} %reduce_sum.702, f32[1,128,12]{1,0,2:T(1,128)S(1)} %reduce_sum.680), channel_id=5, replica_groups=mesh['fsdp'=8,'seq'=4] {'seq'}, use_global_device_ids=true, to_apply=%region_21.22.clone | all-reduce | flops 3072 | bytes 24576
  168.2 11.8 all_gather.71
  180.1 11.9 all_gather.64
  192.0 15.4 %all_gather.70 = f32[1,128,12,64]{1,3,0,2:T(8,128)S(1)} all-gather(f32[1,128,3,64]{1,3,0,2:T(8,128)} %bitcast.876), channel_id=1, replica_groups=mesh['fsdp'=8,'seq'=4] {'seq'}, dimensions={2}, use_global_device_ids=true | all-gather | bytes 491520 | tf_op jit(solution)/shard_map/all_gather | solution.py:121
  210.2 14.8 %all_gather.31 = f32[1,128,12,64]{1,3,0,2:T(8,128)S(1)} all-gather(f32[1,128,3,64]{1,3,0,2:T(8,128)} %bitcast.877), channel_id=1, replica_groups=mesh['fsdp'=8,'seq'=4] {'seq'}, dimensions={2}, use_global_device_ids=true | all-gather | bytes 491520 | tf_op jit(solution)/shard_map/all_gather | solution.py:121
  233.5 52.4 %all-gather.14.cloned.1.call-done = bf16[2,3072,768]{2,1,0:T(8,128)(2,1)} async-done(((bf16[2,384,768]{2,1,0:T(8,128)(2,1)}), bf16[2,3072,768]{2,1,0:T(8,128)(2,1)}) %all-gather.14.cloned.1.call-update) | async-done | bytes 9437200 | tf_op jit(solution)/shard_map/all_gather | solution.py:219
  323.8 5.6 convert_reduce_fusion.2
  370.8 5.5 convert_reduce_fusion.3
  392.7 7.5 convolution_convert_fusion
  400.3 6.2 fusion.1
  410.5 5.5 multiply_convert_fusion
  423.8 7.5 convolution_convert_fusion.1
  431.3 6.1 fusion.3
  464.1 10.5 fusion.75
  474.6 7.2 fusion.74
  490.4 14.1 %all_gather.73 = bf16[1,128,12,64]{1,3,0,2:T(8,128)(2,1)S(1)} all-gather(bf16[1,128,3,64]{1,3,0,2:T(8,128)(2,1)} %bitcast.889), channel_id=1, replica_groups=mesh['fsdp'=8,'seq'=4] {'seq'}, dimensions={2}, use_global_device_ids=true | all-gather | bytes 245760 | tf_op jit(solution)/shard_map/all_gather | solution.py:165
  504.5 14.1 %all_gather.72 = bf16[1,128,12,64]{1,3,0,2:T(8,128)(2,1)S(1)} all-gather(bf16[1,128,3,64]{1,3,0,2:T(8,128)(2,1)} %bitcast.890), channel_id=1, replica_groups=mesh['fsdp'=8,'seq'=4] {'seq'}, dimensions={2}, use_global_device_ids=true | all-gather | bytes 245760 | tf_op jit(solution)/shard_map/all_gather | solution.py:165
  524.4 7.2 maximum_bitcast_fusion.1
  531.6 9.0 maximum_add_fusion.2
  540.6 21.6 %copy.326 = f32[2,3,768,768]{3,0,1,2:T(2,128)} copy(f32[2,3,768,768]{2,3,1,0:T(8,128)} %maximum_add_fusion.2) | data formatting | bytes 28311552 | tf_op jit(solution)/shard_map/add | solution.py:304
  585.9 6.6 fusion.38
  592.6 11.7 bitcast_reduce_fusion.3
  604.7 9.0 fusion.17
  634.1 117.9 %all-reduce.10.cloned.1.call-done = f32[2,3,768,768]{3,0,1,2:T(2,128)} async-done(((f32[2,3,768,768]{3,0,1,2:T(2,128)}), f32[2,3,768,768]{3,0,1,2:T(2,128)}) %all-reduce.10.cloned.1.call-update) | async-done | bytes 14155792
  756.3 5.1 maximum_add_fusion.3
  768.4 5.3 convolution_bitcast_fusion.5
  773.7 11.3 maximum_add_fusion
  792.3 5.3 convolution_bitcast_fusion.1
  797.6 11.8 maximum_add_fusion.1
  810.0 8.2 add_bitcast_fusion.1
  821.3 53.8 %copy.327 = f32[2,1,1578,768]{3,1,2,0:T(1,128)} copy(f32[2,1,1578,768]{3,2,1,0:T(8,128)S(1)} %pad_maximum_fusion) | data formatting | bytes 19390464
  886.8 18.8 %reduce-scatter.36.cloned.1.call-done = f32[96,5]{1,0:T(8,128)} async-done(((f32[768,5]{1,0:T(8,128)}), f32[96,5]{1,0:T(8,128)}) %reduce-scatter.36.cloned.1.call-update) | async-done | bytes 1936
  906.5 11.7 all-reduce.4
  920.4 26.9 %all-reduce.8.cloned.1.call-done = bf16[1,2,96,768]{3,0,1,2:T(2,128)(2,1)} async-done(((bf16[1,2,96,768]{3,0,1,2:T(2,128)(2,1)}), bf16[1,2,96,768]{3,0,1,2:T(2,128)(2,1)}) %all-reduce.8.cloned.1.call-update) | async-done | bytes 294928 | tf_op jit(solution)/shard_map/psum | solution.py:316
  949.0 5.8 scatter.10
  956.2 49.0 %reduce-scatter.28.cloned.1.call-done = f32[2,96,768]{2,1,0:T(8,128)} async-done(((f32[2,768,768]{2,1,0:T(8,128)}), f32[2,96,768]{2,1,0:T(8,128)}) %reduce-scatter.28.cloned.1.call-update) | async-done | bytes 589840 | tf_op jit(solution)/shard_map/reduce_scatter | solution.py:307
  1005.2 130.2 %reduce-scatter.30.cloned.1.call-done = f32[2,96,3072]{2,1,0:T(8,128)} async-done(((f32[2,768,3072]{2,1,0:T(8,128)}), f32[2,96,3072]{2,1,0:T(8,128)}) %reduce-scatter.30.cloned.1.call-update) | async-done | bytes 2359312 | tf_op jit(solution)/shard_map/reduce_scatter | solution.py:308
  1135.4 130.2 %reduce-scatter.32.cloned.1.call-done = f32[2,384,768]{2,1,0:T(8,128)} async-done(((f32[2,3072,768]{2,1,0:T(8,128)}), f32[2,384,768]{2,1,0:T(8,128)}) %reduce-scatter.32.cloned.1.call-update) | async-done | bytes 2359312 | tf_op jit(solution)/shard_map/reduce_scatter | solution.py:309
  (807 shorter events, 296.1 us)
Async XLA Ops:
  7.2 54.4 %all-gather.8.cloned.1.call-start = ((), (), s32[]{:S(2)}) async-start(), calls=%async_computation.11 | async-start | bytes 7962624 | tf_op jit(solution)/shard_map/all_gather | solution.py:216
  7.9 184.1 %reduce-scatter.22.cloned.1.call-start = ((), (), s32[]{:S(2)}) async-start(), calls=%async_computation.16 | async-start | bytes 491520 | tf_op jit(solution)/shard_map/reduce_scatter | solution.py:117
  30.2 56.1 %copy-start.157 = (pred[1578]{0:T(1024)(128)(4,1)}, pred[1578]{0:T(1024)(128)(4,1)S(1)}, u32[]{:S(2)}) copy-start(pred[1578]{0:T(1024)(128)(4,1)S(1)} %fusion.235) | copy-start | bytes 4738
  30.3 67.2 %copy-start.186 = (f32[768]{0:T(1024)}, f32[768]{0:T(1024)S(1)}, u32[]{:S(2)}) copy-start(f32[768]{0:T(1024)S(1)} %get-tuple-element.153) | copy-start | bytes 9220
  30.3 267.9 %copy-start.123 = (f32[768]{0:T(1024)}, f32[768]{0:T(1024)S(1)}, u32[]{:S(2)}) copy-start(f32[768]{0:T(1024)S(1)} %get-tuple-element.151) | copy-start | bytes 9220
  30.3 289.6 %copy-start.125 = (f32[768]{0:T(1024)}, f32[768]{0:T(1024)S(1)}, u32[]{:S(2)}) copy-start(f32[768]{0:T(1024)S(1)} %get-tuple-element.149) | copy-start | bytes 9220
  30.3 306.5 %copy-start.121 = (f32[768]{0:T(1024)}, f32[768]{0:T(1024)S(1)}, u32[]{:S(2)}) copy-start(f32[768]{0:T(1024)S(1)} %get-tuple-element.270) | copy-start | bytes 9220
  31.5 47.9 %copy-start.139 = (f32[128]{0:T(128)}, f32[128]{0:T(128)S(1)}, u32[]{:S(2)}) copy-start(f32[128]{0:T(128)S(1)} %get-tuple-element.271) | copy-start | bytes 1540
  32.8 62.1 %copy-start.215 = (f32[128]{0:T(128)}, f32[128]{0:T(128)S(1)}, u32[]{:S(2)}) copy-start(f32[128]{0:T(128)S(1)} %get-tuple-element.140) | copy-start | bytes 1540
  32.8 46.6 %copy-start.177 = (f32[128]{0:T(128)}, f32[128]{0:T(128)S(1)}, u32[]{:S(2)}) copy-start(f32[128]{0:T(128)S(1)} %fusion.242) | copy-start | bytes 1540
  46.0 22.0 %copy-start.133 = (f32[1578]{0:T(1024)}, f32[1578]{0:T(1024)S(1)}, u32[]{:S(2)}) copy-start(f32[1578]{0:T(1024)S(1)} %fusion.24) | copy-start | bytes 18940
  92.8 115.4 %all-gather.10.cloned.1.call-start = ((), (), s32[]{:S(2)}) async-start(), calls=%async_computation.13 | async-start | bytes 2654208 | tf_op jit(solution)/shard_map/all_gather | solution.py:217
  93.5 116.7 %reduce-scatter.20.cloned.1.call-start = ((), (), s32[]{:S(2)}) async-start(), calls=%async_computation.12 | async-start | bytes 491520 | tf_op jit(solution)/shard_map/reduce_scatter | solution.py:117
  94.9 27.8 %copy-start.159 = (pred[1578]{0:T(1024)(128)(4,1)}, pred[1578]{0:T(1024)(128)(4,1)S(1)}, u32[]{:S(2)}) copy-start(pred[1578]{0:T(1024)(128)(4,1)S(1)} %fusion.234) | copy-start | bytes 4738
  129.1 100.0 %all-gather.12.cloned.1.call-start = ((), (), s32[]{:S(2)}) async-start(), calls=%async_computation.14 | async-start | bytes 10616832 | tf_op jit(solution)/shard_map/all_gather | solution.py:218
  129.7 156.2 %all-gather.14.cloned.1.call-start = ((), (), s32[]{:S(2)}) async-start(), calls=%async_computation.15 | async-start | bytes 10616832 | tf_op jit(solution)/shard_map/all_gather | solution.py:219
  130.3 360.1 %reduce-scatter.26.cloned.1.call-start = ((), (), s32[]{:S(2)}) async-start(), calls=%async_computation.18 | async-start | bytes 245760 | tf_op jit(solution)/shard_map/reduce_scatter | solution.py:162
  149.6 79.5 %copy-start.146 = (f32[1,3072]{1,0:T(1,128)}, f32[1,3072]{1,0:T(1,128)S(1)}, u32[]{:S(2)}) copy-start(f32[1,3072]{1,0:T(1,128)S(1)} %get-tuple-element.199) | copy-start | bytes 36868
  210.0 75.9 %copy-start.19 = (f32[128,768]{1,0:T(8,128)}, f32[128,768]{1,0:T(8,128)S(1)}, u32[]{:S(2)}) copy-start(f32[128,768]{1,0:T(8,128)S(1)} %get-tuple-element.232) | copy-start | bytes 1179652
  210.0 23.5 %copy-start.148 = (f32[128]{0:T(128)}, f32[128]{0:T(128)S(1)}, u32[]{:S(2)}) copy-start(f32[128]{0:T(128)S(1)} %broadcast_multiply_fusion.4) | copy-start | bytes 1540
  227.6 70.6 %copy-start.150 = (f32[128]{0:T(128)}, f32[128]{0:T(128)S(1)}, u32[]{:S(2)}) copy-start(f32[128]{0:T(128)S(1)} %broadcast_multiply_fusion.8) | copy-start | bytes 1540
  229.1 56.8 %copy-start.188 = (f32[768]{0:T(1024)S(1)}, f32[768]{0:T(1024)}, u32[]{:S(2)}) copy-start(f32[768]{0:T(1024)} %get-tuple-element.155) | copy-start | bytes 9220
  296.8 40.0 %copy-start.13 = (f32[128,768]{1,0:T(8,128)}, f32[128,768]{1,0:T(8,128)S(1)}, u32[]{:S(2)}) copy-start(f32[128,768]{1,0:T(8,128)S(1)} %get-tuple-element.238) | copy-start | bytes 1179652
  316.3 20.6 %copy-start.16 = (f32[128,768]{1,0:T(8,128)}, f32[128,768]{1,0:T(8,128)S(1)}, u32[]{:S(2)}) copy-start(f32[128,768]{1,0:T(8,128)S(1)} %get-tuple-element.246) | copy-start | bytes 1179652
  316.3 20.6 %copy-start.155 = (f32[128]{0:T(128)}, f32[128]{0:T(128)S(1)}, u32[]{:S(2)}) copy-start(f32[128]{0:T(128)S(1)} %broadcast_multiply_fusion.6) | copy-start | bytes 1540
  316.5 20.4 %copy-start.169 = (f32[128]{0:T(128)}, f32[128]{0:T(128)S(1)}, u32[]{:S(2)}) copy-start(f32[128]{0:T(128)S(1)} %fusion.241) | copy-start | bytes 1540
  416.0 88.4 %reduce-scatter.24.cloned.1.call-start = ((), (), s32[]{:S(2)}) async-start(), calls=%async_computation.17 | async-start | bytes 245760 | tf_op jit(solution)/shard_map/reduce_scatter | solution.py:162
  463.6 288.4 %all-reduce.10.cloned.1.call-start = ((), (), s32[]{:S(2)}) async-start(), calls=%async_computation.27 | async-start | bytes 28311552
  486.1 32.5 %copy-start.182 = (f32[128]{0:T(128)S(1)}, f32[128]{0:T(128)}, u32[]{:S(2)}) copy-start(f32[128]{0:T(128)} %copy-done.181) | copy-start | bytes 1540
  490.4 28.9 %copy-start.140 = (f32[128]{0:T(128)S(1)}, f32[128]{0:T(128)}, u32[]{:S(2)}) copy-start(f32[128]{0:T(128)} %copy-done.139) | copy-start | bytes 1540
  490.4 28.9 %copy-start.178 = (f32[128]{0:T(128)S(1)}, f32[128]{0:T(128)}, u32[]{:S(2)}) copy-start(f32[128]{0:T(128)} %copy-done.177) | copy-start | bytes 1540
  562.3 319.3 %reduce-scatter.40.cloned.1.call-start = ((), (), s32[]{:S(2)}) async-start(), calls=%async_computation.26 | async-start | bytes 442368
  604.4 278.6 %reduce-scatter.38.cloned.1.call-start = ((), (), s32[]{:S(2)}) async-start(), calls=%async_computation.25 | async-start | bytes 1769472
  617.7 268.3 %reduce-scatter.34.cloned.1.call-start = ((), (), s32[]{:S(2)}) async-start(), calls=%async_computation.23 | async-start | bytes 442368
  624.6 130.0 %copy-start.109 = (bf16[12,64,128]{2,1,0:T(8,128)(2,1)S(1)}, bf16[12,64,128]{2,1,0:T(8,128)(2,1)}, u32[]{:S(2)}) copy-start(bf16[12,64,128]{2,1,0:T(8,128)(2,1)} %copy-done.108) | copy-start | bytes 589828
  624.6 130.0 %copy-start.115 = (bf16[128,768]{1,0:T(8,128)(2,1)S(1)}, bf16[128,768]{1,0:T(8,128)(2,1)}, u32[]{:S(2)}) copy-start(bf16[128,768]{1,0:T(8,128)(2,1)} %copy-done.114) | copy-start | bytes 589828
  624.6 281.0 %reduce-scatter.36.cloned.1.call-start = ((), (), s32[]{:S(2)}) async-start(), calls=%async_computation.24 | async-start | bytes 442368
  634.1 313.2 %all-reduce.8.cloned.1.call-start = ((), (), s32[]{:S(2)}) async-start(), calls=%async_computation.19 | async-start | bytes 1179648 | tf_op jit(solution)/shard_map/psum | solution.py:316
  754.5 250.6 %reduce-scatter.28.cloned.1.call-start = ((), (), s32[]{:S(2)}) async-start(), calls=%async_computation.20 | async-start | bytes 5308416 | tf_op jit(solution)/shard_map/reduce_scatter | solution.py:307
  761.5 373.9 %reduce-scatter.30.cloned.1.call-start = ((), (), s32[]{:S(2)}) async-start(), calls=%async_computation.21 | async-start | bytes 21233664 | tf_op jit(solution)/shard_map/reduce_scatter | solution.py:308
  785.0 480.6 %reduce-scatter.32.cloned.1.call-start = ((), (), s32[]{:S(2)}) async-start(), calls=%async_computation.22 | async-start | bytes 21233664 | tf_op jit(solution)/shard_map/reduce_scatter | solution.py:309
  821.2 53.8 %copy-start.15 = (f32[128,768]{1,0:T(8,128)S(1)}, f32[128,768]{1,0:T(8,128)}, u32[]{:S(2)}) copy-start(f32[128,768]{1,0:T(8,128)} %copy-done.13) | copy-start | bytes 1179652
  821.3 53.8 %copy-start.67 = (f32[128,3072]{1,0:T(8,128)S(1)}, f32[128,3072]{1,0:T(8,128)}, u32[]{:S(2)}) copy-start(f32[128,3072]{1,0:T(8,128)} %copy-done.65) | copy-start | bytes 4718596
  821.3 53.8 %copy-start.185 = (f32[768]{0:T(1024)S(1)}, f32[768]{0:T(1024)}, u32[]{:S(2)}) copy-start(f32[768]{0:T(1024)} %get-tuple-element.154) | copy-start | bytes 9220
  821.3 57.4 %slice-start.12 = ((s8[9437184]{0:T(1024)(128)(4,1)}), s8[1048576]{0:T(1024)(128)(4,1)S(1)}, s32[]{:S(2)}) async-start(s8[9437184]{0:T(1024)(128)(4,1)} %bitcast.909), calls=%async_computation.40 | async-start | bytes 2097152
  821.3 57.4 %slice-start.13 = ((s8[9437184]{0:T(1024)(128)(4,1)}), s8[4194304]{0:T(1024)(128)(4,1)S(1)}, s32[]{:S(2)}) async-start(s8[9437184]{0:T(1024)(128)(4,1)} %bitcast.909), calls=%async_computation.41 | async-start | bytes 8388608
  918.3 36.5 %copy-start.137 = (f32[5,96]{1,0:T(8,128)}, f32[5,96]{1,0:T(8,128)S(1)}, u32[]{:S(2)}) copy-start(f32[5,96]{1,0:T(8,128)S(1)} %scatter.11) | copy-start | bytes 5764
  918.3 36.5 %copy-start.138 = (f32[5,96]{1,0:T(8,128)}, f32[5,96]{1,0:T(8,128)S(1)}, u32[]{:S(2)}) copy-start(f32[5,96]{1,0:T(8,128)S(1)} %scatter.14) | copy-start | bytes 5764
  (222 other events, 1076.3 us)
Sparse Core Ops, SparseCore 0:
  9.9 51.5 all-gather.7
  92.9 20.5 reduce-scatter.21
  115.6 27.2 all-gather.9
  145.7 20.6 reduce-scatter.19
  168.2 56.9 all-gather.11
  227.0 58.8 all-gather.13
  416.2 19.3 reduce-scatter.25
  463.7 19.4 reduce-scatter.23
  562.4 189.5 all-reduce.9
  755.2 33.9 reduce-scatter.39
  792.9 38.4 reduce-scatter.37
  834.6 33.7 reduce-scatter.33
  871.7 33.8 reduce-scatter.35
  908.0 39.3 all-reduce.7
  951.6 53.5 reduce-scatter.27
  1009.2 126.1 reduce-scatter.29
  1139.4 126.1 reduce-scatter.31
where the time goes:
time: 1280 us; the launch traced here: 1270 us
  waiting for transfers between devices  544 us (42%)
  matrix products  246 us (19%)
  local copies, waits for them, and re-layouts  220 us (17%)
  blocking collectives  148 us (12%)
  other arithmetic  91.5 us (7%)
  between operations  20.5 us (2%)
    dot_general x78, matrix products, product(): return jnp.einsum(form, left, right, preferred_element_type=jnp.float32)  246 us
    unnamed x22, waiting for transfers between devices  139 us
    reduce_scatter x1, waiting for transfers between devices, per_device(): lax.psum_scatter(grad_sum[2], 'fsdp', scatter_dimension=1, tiled=True)  130 us
    reduce_scatter x1, waiting for transfers between devices, per_device(): lax.psum_scatter(grad_sum[3], 'fsdp', scatter_dimension=1, tiled=True)  130 us
    unnamed x525, local copies, waits for them, and re-layouts  90.3 us
    all_gather x1, waiting for transfers between devices, per_device(): lax.all_gather(mlp_out, 'fsdp', axis=1, tiled=True)  52.4 us
    reduce_scatter x1, waiting for transfers between devices, per_device(): lax.psum_scatter(grad_sum[1], 'fsdp', scatter_dimension=1, tiled=True)  49 us
    add x8, other arithmetic, per_device(): jax.tree.map(jnp.add, grad_sum, grad_step)  37.3 us
  transfers between devices with their start and end apart: 17, of which 8 were waited for; matrix products, arithmetic and copies ran while one was open for 27% of the time, Pallas kernels for 0%

commit v1 on v0

v1 whole, which is shorter than its diff:
```python
import functools

import jax
import jax.numpy as jnp
from jax import lax
from jax.experimental import pallas as pl
from jax.experimental.pallas import tpu as pltpu
from jax.sharding import PartitionSpec as P

D = 768
HEADS = 12
HEAD = 64
PAIRS = HEADS // 2
FF = 3072
NLAT = 128
PATCHES = 392
FRAMES = 16
OWNERS = 8
SHARE = D // OWNERS
CHUNKS = FF // D
HALF = D // 2
PAY = D + 128
VEC_F = 16
VEC_S = 32
VEC_K = 32
ROWS_F = CHUNKS * SHARE + CHUNKS * SHARE + VEC_F
ROWS_S = 2 * CHUNKS * SHARE + 5 * SHARE + VEC_S
ROWS_K = 3 * SHARE + VEC_K
EPS = 1e-06
F32 = jnp.float32
BF = jnp.bfloat16
GELU_C = 0.7978845608028654
GELU_A = 0.044715
VMEM_CAP = 60 * 1024 * 1024


def nn(a, b):
    return lax.dot_general(a, b, (((1,), (0,)), ((), ())), preferred_element_type=F32)


def nt(a, b):
    return lax.dot_general(a, b, (((1,), (1,)), ((), ())), preferred_element_type=F32)


def tn(a, b):
    return lax.dot_general(a, b, (((0,), (0,)), ((), ())), preferred_element_type=F32)


def ln_parts(x):
    center = x - jnp.mean(x, -1, keepdims=True)
    rstd = lax.rsqrt(jnp.mean(center * center, -1, keepdims=True) + EPS)
    return center, rstd


def ln(x, gain, bias):
    center, rstd = ln_parts(x)
    return center * rstd * gain + bias


def ln_back(x, gain, grad):
    center, rstd = ln_parts(x)
    xhat = center * rstd
    dx = grad * gain
    back = rstd * (dx - jnp.mean(dx, -1, keepdims=True) - xhat * jnp.mean(dx * xhat, -1, keepdims=True))
    return back, grad * xhat


def gelu(h):
    return h * (0.5 * (1.0 + jnp.tanh(GELU_C * (h + GELU_A * h * h * h))))


def gelu_both(h):
    square = h * h
    t = jnp.tanh(GELU_C * (h + GELU_A * h * square))
    cdf = 0.5 * (1.0 + t)
    slope = cdf + 0.5 * h * (1.0 - t * t) * (GELU_C * (1.0 + 3.0 * GELU_A * square))
    return h * cdf, slope


def low_lanes(rows):
    return lax.broadcasted_iota(jnp.int32, (rows, 128), 1) < HEAD


def block_diag(pair):
    wide = pair.astype(F32)
    low = low_lanes(pair.shape[0])
    return jnp.concatenate([jnp.where(low, wide, 0.0), jnp.where(low, 0.0, wide)], 0).astype(BF)


def diag_of(both):
    rows = both.shape[0] // 2
    return jnp.where(low_lanes(rows), both[:rows], both[rows:])


class Pack:
    def __init__(self, arrays, where):
        self.arrays, self.where = arrays, where

    def start(self, refs, row, rows, place, f, sem):
        for m in range(OWNERS):
            index, lead, first = self.where(m, row)
            src = refs[index] if lead is None else refs[index].at[lead]
            pltpu.make_async_copy(src.at[pl.ds(first, rows)], place(f ^ m), sem).start()


def wait_for(ref, sem):
    pltpu.make_async_copy(ref, ref, sem).wait()


def share_rows(ref, g, first=0, span=SHARE, step=SHARE):
    return ref.at[pl.ds(pl.multiple_of(g * step + first, SHARE), span)]


def start_square(pack, refs, row, dst, f, sem):
    pack.start(refs, row, SHARE, lambda g: share_rows(dst, g), f, sem)


def start_up(pack, refs, row, dst, f, sems):
    for t in range(CHUNKS):
        lanes = pl.ds(t * D, D)
        pack.start(
            refs,
            row + t * SHARE,
            SHARE,
            lambda g, lanes=lanes: dst.at[pl.ds(pl.multiple_of(g * SHARE, SHARE), SHARE), lanes],
            f,
            sems.at[t],
        )


def start_down(pack, refs, row, dst, f, sem):
    for t in range(CHUNKS):
        pack.start(
            refs,
            row + t * SHARE,
            SHARE,
            lambda g, t=t: share_rows(dst, g, t * SHARE, SHARE, CHUNKS * SHARE),
            f,
            sem,
        )


ANY = pl.BlockSpec(memory_space=pl.ANY)
WHOLE = pl.BlockSpec(memory_space=pltpu.VMEM)


def sds(shape, dtype):
    return jax.ShapeDtypeStruct(shape, dtype)


def cost(flops, size, exps=0):
    return pl.CostEstimate(flops=int(flops), bytes_accessed=int(size), transcendentals=int(exps))


PARAMS = pltpu.CompilerParams(vmem_limit_bytes=VMEM_CAP)


def keyval_kernel(pack, local, tile, meta, x_ref, *refs):
    count = len(pack.arrays)
    wrefs, (xl_ref, k_ref, v_ref, gb_ref, bin_ref, wkv, small, sems) = refs[:count], refs[count:]
    f = meta[0]

    @pl.when((pl.program_id(0) == 0) & (pl.program_id(1) == 0))
    def _():
        for m in range(OWNERS):
            index, lead, first = pack.where(m, 2 * SHARE)
            src = wrefs[index] if lead is None else wrefs[index].at[lead]
            pltpu.make_async_copy(
                src.at[pl.ds(first, 16), pl.ds(0, 256)], small.at[m], sems.at[2]
            ).start()
        start_square(pack, wrefs, 0, wkv.at[0], f, sems.at[0])
        start_square(pack, wrefs, SHARE, wkv.at[1], f, sems.at[1])
        wait_for(small, sems.at[2])
        lane = lax.broadcasted_iota(jnp.int32, (128, D), 1)
        row = lax.broadcasted_iota(jnp.int32, (128, D), 0)
        total = jnp.zeros((16, D), F32)
        for m in range(OWNERS):
            g = f ^ m
            place = jnp.where((lane - g * SHARE == row) & (row < SHARE), 1.0, 0.0).astype(BF)
            total = total + nn(small[m, :, 0:128], place)
            wide = small[m].astype(F32)
            for u in range(6):
                i, part = u // 3, u % 3
                line = wide[12 + u : 13 + u, 0:128] if u < 4 else wide[u - 4 : u - 3, 128:256]
                at = pl.ds(pl.multiple_of((3 * g + part) * 128, 128), 128)
                bin_ref[i : i + 1, at] = line
        gb_ref[...] = total
        wait_for(wkv.at[0], sems.at[0])
        wait_for(wkv.at[1], sems.at[1])

    x = x_ref[0].astype(F32)
    normed = ln(x, gb_ref[1:2], gb_ref[6:7])
    row = pl.program_id(1) * tile + lax.broadcasted_iota(jnp.int32, (tile, D), 0)
    xl = jnp.where(row < local, normed, 0.0).astype(BF)
    xl_ref[0] = xl
    k_ref[0] = nn(xl, wkv[0]).astype(BF)
    v_ref[0] = nn(xl, wkv[1]).astype(BF)


def keyval(pack, meta, tokens, local, padded):
    clips = tokens.shape[0]
    tile = padded // 4
    block = pl.BlockSpec((1, tile, D), lambda i, j, m: (i, j, 0))
    fixed = lambda shape: pl.BlockSpec(shape, lambda i, j, m: (0,) * len(shape))
    return pl.pallas_call(
        functools.partial(keyval_kernel, pack, local, tile),
        grid_spec=pltpu.PrefetchScalarGridSpec(
            num_scalar_prefetch=1,
            grid=(clips, padded // tile),
            in_specs=[block] + [ANY] * len(pack.arrays),
            out_specs=[block, block, block, fixed((16, D)), fixed((2, FF))],
            scratch_shapes=[
                pltpu.VMEM((2, D, D), BF),
                pltpu.VMEM((OWNERS, 16, 256), BF),
                pltpu.SemaphoreType.DMA((3,)),
            ],
        ),
        out_shape=[sds((clips, padded, D), BF)] * 3 + [sds((16, D), F32), sds((2, FF), F32)],
        compiler_params=PARAMS,
        cost_estimate=cost(4 * clips * padded * D * D, clips * padded * D * 8),
        name="keyval",
    )(meta, tokens, *pack.arrays)


def spans(total, step):
    return [(at, min(step, total - at)) for at in range(0, total, step)]


def attend_kernel(pack, padded, meta, lat_ref, gb_ref, bias_ref, k_ref, v_ref, *refs):
    count = len(pack.arrays)
    wrefs, (pay_ref, q_ref, wq, qs, lv, sem) = refs[:count], refs[count:]
    f = meta[0]
    clip, pair = pl.program_id(0), pl.program_id(1)

    @pl.when((clip == 0) & (pair == 0))
    def _():
        start_square(pack, wrefs, 0, wq, f, sem.at[0])
        zl = ln(lat_ref[...].astype(F32), gb_ref[0:1], gb_ref[5:6]).astype(BF)
        wait_for(wq, sem.at[0])
        q = nn(zl, wq[...]).astype(BF).astype(F32) * 0.125
        qs[...] = q.astype(BF)
        q_ref[...] = qs[...]

    at = pl.ds(pl.multiple_of(pair * 128, 128), 128)
    rows = pl.ds(pl.multiple_of(clip * NLAT, NLAT), NLAT)
    qbd = block_diag(qs[rows, at])
    lsum = jnp.zeros((2 * NLAT, 128), F32)
    u = jnp.zeros((2 * NLAT, 128), F32)
    for first, width in spans(padded, 256):
        s = nt(qbd, k_ref[0, first : first + width, :])
        e = jnp.exp(s + bias_ref[0, :, first : first + width])
        for part in range(0, width, 128):
            lsum = lsum + e[:, part : part + 128]
        u = u + nn(e.astype(BF), v_ref[0, first : first + width, :])
    pay_ref[0, :, at] = diag_of(u).astype(BF)
    l = jnp.sum(lsum, -1, keepdims=True)
    lane = lax.broadcasted_iota(jnp.int32, (NLAT, 128), 1)
    old = jnp.where(pair == 0, 0.0, lv[...])
    new = jnp.where(lane == 2 * pair, l[:NLAT], jnp.where(lane == 2 * pair + 1, l[NLAT:], old))
    lv[...] = new

    @pl.when(pair == PAIRS - 1)
    def _():
        pay_ref[0, :, D:PAY] = split_pair(lv[...])


def split_pair(values):
    high = values.astype(BF).astype(F32)
    rest = values - high
    return jnp.where(low_lanes(values.shape[0]), high, pltpu.roll(rest, HEAD, 1)).astype(BF)


def join_pair(pay):
    wide = pay.astype(F32)
    return wide + pltpu.roll(wide, HEAD, 1)


def attend(pack, meta, lat, gb, bias, k, v):
    clips, padded = k.shape[0], k.shape[1]
    rows = lat.shape[0]
    fixed = lambda shape: pl.BlockSpec(shape, lambda i, j, m: (0,) * len(shape))
    lanes = pl.BlockSpec((1, padded, 128), lambda i, j, m: (i, 0, j))
    return pl.pallas_call(
        functools.partial(attend_kernel, pack, padded),
        grid_spec=pltpu.PrefetchScalarGridSpec(
            num_scalar_prefetch=1,
            grid=(clips, PAIRS),
            in_specs=[
                fixed((rows, D)),
                fixed((16, D)),
                pl.BlockSpec((1, 1, padded), lambda i, j, m: (i, 0, 0)),
                lanes,
                lanes,
            ]
            + [ANY] * len(pack.arrays),
            out_specs=[
                pl.BlockSpec((1, NLAT, PAY), lambda i, j, m: (i, 0, 0)),
                fixed((rows, D)),
            ],
            scratch_shapes=[
                pltpu.VMEM((D, D), BF),
                pltpu.VMEM((rows, D), BF),
                pltpu.VMEM((NLAT, 128), F32),
                pltpu.SemaphoreType.DMA((1,)),
            ],
        ),
        out_shape=[sds((clips, NLAT, PAY), BF), sds((rows, D), BF)],
        compiler_params=PARAMS,
        cost_estimate=cost(
            8 * clips * padded * NLAT * D, clips * padded * D * 4, clips * padded * NLAT * HEADS
        ),
        name="attend",
    )(meta, lat, gb, bias, k, v, *pack.arrays)


def combine_kernel(*refs):
    parts, out_ref = refs[1:-1], refs[-1]
    total = parts[0][...].astype(F32)
    for part in parts[1:]:
        total = total + part[...].astype(F32)
    l = total[:, D:PAY]
    l = l + pltpu.roll(l, HEAD, 1)
    low = low_lanes(total.shape[0])
    for j in range(PAIRS):
        den = jnp.where(low, l[:, 2 * j : 2 * j + 1], l[:, 2 * j + 1 : 2 * j + 2])
        out_ref[:, 128 * j : 128 * j + 128] = (total[:, 128 * j : 128 * j + 128] / den).astype(BF)
    out_ref[:, D:PAY] = split_pair(l)


def combine(meta, pay, received):
    rows = received[0].shape[0] if received else pay.shape[0]
    fixed = pl.BlockSpec((rows, PAY), lambda i, m: (0, 0))
    return pl.pallas_call(
        combine_kernel,
        grid_spec=pltpu.PrefetchScalarGridSpec(
            num_scalar_prefetch=1,
            grid=(1,),
            in_specs=[pl.BlockSpec((rows, PAY), lambda i, m: (m[1], 0))] + [fixed] * len(received),
            out_specs=fixed,
        ),
        out_shape=sds((rows, PAY), BF),
        name="combine",
    )(meta, pay, *received)


def first_kernel(wo_pack, ff_pack, count, meta, *refs):
    parts = refs[:count]
    lat_ref, gb_ref, bin_ref = refs[count : count + 3]
    refs = refs[count + 3 :]
    n_wo, n_ff = len(wo_pack.arrays), len(ff_pack.arrays)
    wo_refs, ff_refs, refs = refs[:n_wo], refs[n_wo : n_wo + n_ff], refs[n_wo + n_ff :]
    o_ref, l_ref, z1_ref, z2_ref, h_ref, wo, win, wout, hs, sems, hsems = refs
    f, s = meta[0], meta[1]
    start_square(wo_pack, wo_refs, SHARE, wo, f, sems.at[0])
    start_up(ff_pack, ff_refs, 0, win, f, sems.at[pl.ds(1, CHUNKS)])
    start_down(ff_pack, ff_refs, CHUNKS * SHARE, wout, f, sems.at[1 + CHUNKS])
    step = parts[0].shape[0]
    for k, part in enumerate(parts):
        rows = pl.ds(pl.multiple_of(lax.rem(s - k + count, count) * step, step), step)
        o_ref[rows, :] = part[:, :D]
        l_ref[rows, :] = join_pair(part[:, D:PAY])
    wait_for(wo, sems.at[0])
    z1 = lat_ref[...].astype(F32) + nn(o_ref[...], wo[...])
    z1_ref[...] = z1
    n = ln(z1, gb_ref[2:3], gb_ref[7:8]).astype(BF)
    y = jnp.zeros_like(z1)
    for c in range(CHUNKS):
        at = slice(c * D, c * D + D)
        wait_for(win.at[:, at], sems.at[1 + c])
        h = nn(n, win[:, at]) + bin_ref[0:1, at]
        hs[:, at] = h
        pltpu.make_async_copy(hs.at[:, at], h_ref.at[:, at], hsems.at[c]).start()
        a = gelu(h).astype(BF)
        if c == 0:
            wait_for(wout, sems.at[1 + CHUNKS])
        y = y + nn(a, wout[at, :])
    z2_ref[...] = z1 + (y + gb_ref[10:11])
    for c in range(CHUNKS):
        at = slice(c * D, c * D + D)
        pltpu.make_async_copy(hs.at[:, at], h_ref.at[:, at], hsems.at[c]).wait()


def first_block(wo_pack, ff_pack, meta, parts, lat, gb, bins):
    rows = lat.shape[0]
    n_w = len(wo_pack.arrays) + len(ff_pack.arrays)
    return pl.pallas_call(
        functools.partial(first_kernel, wo_pack, ff_pack, len(parts)),
        in_specs=[pl.BlockSpec(memory_space=pltpu.SMEM)] + [WHOLE] * (len(parts) + 3) + [ANY] * n_w,
        out_specs=[WHOLE] * 4 + [ANY],
        scratch_shapes=[
            pltpu.VMEM((D, D), BF),
            pltpu.VMEM((D, FF), BF),
            pltpu.VMEM((FF, D), BF),
            pltpu.VMEM((rows, FF), F32),
            pltpu.SemaphoreType.DMA((2 + CHUNKS,)),
            pltpu.SemaphoreType.DMA((CHUNKS,)),
        ],
        out_shape=[
            sds((rows, D), BF),
            sds((rows, 128), F32),
            sds((rows, D), F32),
            sds((rows, D), F32),
            sds((rows, FF), F32),
        ],
        compiler_params=PARAMS,
        cost_estimate=cost(18 * rows * D * D, 16 * D * D * 2),
        name="first_block",
    )(meta, *parts, lat, gb, bins, *wo_pack.arrays, *ff_pack.arrays)


def softmax_rows(scores):
    e = jnp.exp(scores - jnp.max(scores, -1, keepdims=True))
    return e / jnp.sum(e, -1, keepdims=True)


def put_vec(shares, rows, row, width):
    vec = jnp.concatenate(rows + [jnp.zeros((width - len(rows), HALF), F32)], 0).astype(BF)
    for which in range(2):
        for k in range(4):
            shares[which, k, row : row + width, :] = vec


def halves(line):
    return [line[:, i : i + HALF] for i in range(0, line.shape[1], HALF)]


def column_sum(values):
    return jnp.sum(values, 0, keepdims=True)


def put_rows(shares, f, row, grad, first=0):
    grad = grad.astype(BF)
    for g in range(OWNERS):
        rel = f ^ g
        shares[rel & 1, rel >> 1, row : row + SHARE, :] = grad[g * SHARE : g * SHARE + SHARE]


def put_down(shares, f, row, grad, u):
    grad = grad.astype(BF)
    span = CHUNKS * SHARE
    for i in range(D // span):
        rel = f ^ (u * (D // span) + i)
        shares[rel & 1, rel >> 1, row : row + span, :] = grad[i * span : i * span + span]


def ff_grads(shares, f, h, row, n, dh_ref, a_ref, dy_ref):
    for c in range(CHUNKS):
        at = pl.ds(pl.multiple_of(h * (FF // 2) + c * HALF, 128), HALF)
        put_rows(shares, f, row + c * SHARE, tn(n, dh_ref[:, at]))
    dyh = dy_ref[:, pl.ds(pl.multiple_of(h * HALF, 128), HALF)]
    for u in range(CHUNKS):
        put_down(shares, f, row + CHUNKS * SHARE, tn(a_ref[:, u * D : u * D + D], dyh), u)


def send_shares(shares, keep_ref, send_ref, sems):
    copies = [
        pltpu.make_async_copy(shares.at[0], keep_ref, sems.at[0]),
        pltpu.make_async_copy(shares.at[1], send_ref, sems.at[1]),
    ]
    for copy in copies:
        copy.start()
    for copy in copies:
        copy.wait()


def second_kernel(pack, meta, z2_ref, g4_ref, gb_ref, bin_ref, *refs):
    count = len(pack.arrays)
    wrefs, refs = refs[:count], refs[count:]
    out_ref, g3_ref, qkv_ref, o2_ref, keep_ref, send_ref = refs[:6]
    wqkv, wo, win, wout, hs, ac, dhs, shares, sems, osems = refs[6:]
    f, h = meta[0], meta[2]
    for j in range(3):
        start_square(pack, wrefs, j * SHARE, wqkv.at[j], f, sems.at[j])
    start_square(pack, wrefs, 3 * SHARE, wo, f, sems.at[3])
    start_up(pack, wrefs, 4 * SHARE, win, f, sems.at[pl.ds(4, CHUNKS)])
    start_down(pack, wrefs, (4 + CHUNKS) * SHARE, wout, f, sems.at[4 + CHUNKS])
    z2 = z2_ref[...]
    m = ln(z2, gb_ref[3:4], gb_ref[8:9]).astype(BF)
    for j in range(3):
        wait_for(wqkv.at[j], sems.at[j])
        qkv_ref[j] = nn(m, wqkv[j]).astype(BF)
    for clip in range(z2.shape[0] // NLAT):
        rows = slice(clip * NLAT, clip * NLAT + NLAT)
        for pair in range(PAIRS):
            at = slice(pair * 128, pair * 128 + 128)
            p = softmax_rows(nt(block_diag(qkv_ref[0, rows, at]), qkv_ref[1, rows, at]) * 0.125)
            o2_ref[rows, at] = diag_of(nn(p.astype(BF), qkv_ref[2, rows, at])).astype(BF)
    wait_for(wo, sems.at[3])
    z3 = z2 + nn(o2_ref[...], wo[...])
    n = ln(z3, gb_ref[4:5], gb_ref[9:10]).astype(BF)
    y = jnp.zeros_like(z3)
    for c in range(CHUNKS):
        at = slice(c * D, c * D + D)
        wait_for(win.at[:, at], sems.at[4 + c])
        hidden = nn(n, win[:, at]) + bin_ref[1:2, at]
        act, slope = gelu_both(hidden)
        hs[:, at] = slope
        ac[:, at] = act.astype(BF)
        if c == 0:
            wait_for(wout, sems.at[4 + CHUNKS])
        y = y + nn(ac[:, at], wout[at, :])
    out_ref[...] = z3 + (y + gb_ref[11:12])
    dy = g4_ref[...]
    dn = jnp.zeros_like(z3)
    dbin = []
    for c in range(CHUNKS):
        at = slice(c * D, c * D + D)
        dh = (nt(dy, wout[at, :]) * hs[:, at]).astype(BF)
        dhs[:, at] = dh
        dbin += halves(column_sum(dh.astype(F32)))
        dn = dn + nt(dh, win[:, at])
    back, dgain = ln_back(z3, gb_ref[4:5], dn)
    g4 = dy.astype(F32)
    g3_ref[...] = g4 + back
    ff_grads(shares, f, h, 0, n, dhs, ac, g4_ref)
    vec = halves(column_sum(dgain)) + halves(column_sum(dn)) + halves(column_sum(g4)) + dbin
    put_vec(shares, vec, 2 * CHUNKS * SHARE, VEC_F)
    send_shares(shares, keep_ref, send_ref, osems)


def second_block(pack, meta, z2, g4, gb, bins):
    rows = z2.shape[0]
    return pl.pallas_call(
        functools.partial(second_kernel, pack),
        in_specs=[pl.BlockSpec(memory_space=pltpu.SMEM)] + [WHOLE] * 4 + [ANY] * len(pack.arrays),
        out_specs=[WHOLE] * 4 + [ANY] * 2,
        scratch_shapes=[
            pltpu.VMEM((3, D, D), BF),
            pltpu.VMEM((D, D), BF),
            pltpu.VMEM((D, FF), BF),
            pltpu.VMEM((FF, D), BF),
            pltpu.VMEM((rows, FF), F32),
            pltpu.VMEM((rows, FF), BF),
            pltpu.VMEM((rows, FF), BF),
            pltpu.VMEM((2, 4, ROWS_F, HALF), BF),
            pltpu.SemaphoreType.DMA((5 + CHUNKS,)),
            pltpu.SemaphoreType.DMA((2,)),
        ],
        out_shape=[
            sds((rows, D), F32),
            sds((rows, D), F32),
            sds((3, rows, D), BF),
            sds((rows, D), BF),
            sds((4, ROWS_F, HALF), BF),
            sds((4, ROWS_F, HALF), BF),
        ],
        compiler_params=PARAMS,
        cost_estimate=cost(50 * rows * D * D, 12 * D * D * 4),
        name="second_block",
    )(meta, z2, g4, gb, bins, *pack.arrays)


def third_kernel(ff_pack, self_pack, wo_pack, meta, *refs):
    g3_ref, z2_ref, z1_ref, o2_ref, qkv_ref, o_ref, l_ref, gb_ref, h_ref = refs[:9]
    refs = refs[9:]
    sizes = [len(p.arrays) for p in (ff_pack, self_pack, wo_pack)]
    ff_refs, refs = refs[: sizes[0]], refs[sizes[0] :]
    self_refs, refs = refs[: sizes[1]], refs[sizes[1] :]
    wo_refs, refs = refs[: sizes[2]], refs[sizes[2] :]
    g1_ref, du_ref, dl_ref, keep_ref, send_ref = refs[:5]
    wqkv, wo1, wo0, win, wout, hs, ac, dhs, dqkv, dab, dyb, shares, sems, osems = refs[5:]
    f, h = meta[0], meta[2]
    start_square(self_pack, self_refs, 3 * SHARE, wo1, f, sems.at[3])
    for j in range(3):
        start_square(self_pack, self_refs, j * SHARE, wqkv.at[j], f, sems.at[j])
    hcopy = pltpu.make_async_copy(h_ref, hs, sems.at[4])
    hcopy.start()
    start_down(ff_pack, ff_refs, CHUNKS * SHARE, wout, f, sems.at[5])
    start_up(ff_pack, ff_refs, 0, win, f, sems.at[pl.ds(6, CHUNKS)])
    start_square(wo_pack, wo_refs, SHARE, wo0, f, sems.at[6 + CHUNKS])
    half = pl.ds(pl.multiple_of(h * HALF, 128), HALF)

    g3 = g3_ref[...]
    dab[...] = g3.astype(BF)
    wait_for(wo1, sems.at[3])
    dyb[...] = nt(dab[...], wo1[...]).astype(BF)
    for clip in range(g3.shape[0] // NLAT):
        rows = slice(clip * NLAT, clip * NLAT + NLAT)
        for pair in range(PAIRS):
            at = slice(pair * 128, pair * 128 + 128)
            q, k, v = qkv_ref[0, rows, at], qkv_ref[1, rows, at], qkv_ref[2, rows, at]
            qbd = block_diag(q)
            p = softmax_rows(nt(qbd, k) * 0.125)
            dobd = block_diag(dyb[rows, at])
            dp = nt(dobd, v)
            ds = (p * (dp - jnp.sum(p * dp, -1, keepdims=True))).astype(BF)
            dqkv[0, rows, at] = (diag_of(nn(ds, k)) * 0.125).astype(BF)
            dqkv[1, rows, at] = (tn(ds, qbd) * 0.125).astype(BF)
            dqkv[2, rows, at] = tn(p.astype(BF), dobd).astype(BF)
    row = 2 * CHUNKS * SHARE
    put_rows(shares, f, row + 3 * SHARE, tn(o2_ref[...], dab[:, half]))
    z2 = z2_ref[...]
    m = ln(z2, gb_ref[3:4], gb_ref[8:9]).astype(BF)
    dm = jnp.zeros_like(g3)
    for j in range(3):
        wait_for(wqkv.at[j], sems.at[j])
        dm = dm + nt(dqkv[j], wqkv[j])
        put_rows(shares, f, row + j * SHARE, tn(m, dqkv[j, :, half]))
    back, dgain3 = ln_back(z2, gb_ref[3:4], dm)
    g2 = g3 + back

    z1 = z1_ref[...]
    n = ln(z1, gb_ref[2:3], gb_ref[7:8]).astype(BF)
    dyb[...] = g2.astype(BF)
    hcopy.wait()
    wait_for(wout, sems.at[5])
    dn = jnp.zeros_like(g3)
    dbin = []
    for c in range(CHUNKS):
        at = slice(c * D, c * D + D)
        act, slope = gelu_both(hs[:, at])
        ac[:, at] = act.astype(BF)
        dh = (nt(dyb[...], wout[at, :]) * slope).astype(BF)
        dhs[:, at] = dh
        dbin += halves(column_sum(dh.astype(F32)))
        wait_for(win.at[:, at], sems.at[6 + c])
        dn = dn + nt(dh, win[:, at])
    back, dgain2 = ln_back(z1, gb_ref[2:3], dn)
    g1 = g2 + back
    g1_ref[...] = g1
    ff_grads(shares, f, h, 0, n, dhs, ac, dyb)
    vec = halves(column_sum(dgain2)) + halves(column_sum(dn))
    vec += halves(column_sum(dyb[...].astype(F32))) + dbin
    vec += halves(column_sum(dgain3)) + halves(column_sum(dm))
    put_vec(shares, vec, row + 5 * SHARE, VEC_S)

    dab[...] = g1.astype(BF)
    wait_for(wo0, sems.at[6 + CHUNKS])
    do = nt(dab[...], wo0[...]).astype(BF).astype(F32)
    put_rows(shares, f, row + 4 * SHARE, tn(o_ref[...], dab[:, half]))
    low = low_lanes(g3.shape[0])
    lane = lax.broadcasted_iota(jnp.int32, low.shape, 1)
    l = l_ref[...]
    dl = jnp.zeros(low.shape, F32)
    for j in range(PAIRS):
        at = slice(128 * j, 128 * j + 128)
        first, later = l[:, 2 * j : 2 * j + 1], l[:, 2 * j + 1 : 2 * j + 2]
        du_ref[:, at] = (do[:, at] / jnp.where(low, first, later)).astype(BF)
        t = do[:, at] * o_ref[:, at].astype(F32)
        t_first = -jnp.sum(jnp.where(low, t, 0.0), -1, keepdims=True) / first
        t_later = -jnp.sum(jnp.where(low, 0.0, t), -1, keepdims=True) / later
        dl = jnp.where(lane == 2 * j, t_first, jnp.where(lane == 2 * j + 1, t_later, dl))
    dl_ref[...] = dl
    send_shares(shares, keep_ref, send_ref, osems)


def third_block(ff_pack, self_pack, wo_pack, meta, g3, z2, z1, o2, qkv, o, l, gb, hidden):
    rows = z2.shape[0]
    arrays = [*ff_pack.arrays, *self_pack.arrays, *wo_pack.arrays]
    return pl.pallas_call(
        functools.partial(third_kernel, ff_pack, self_pack, wo_pack),
        in_specs=[pl.BlockSpec(memory_space=pltpu.SMEM)]
        + [WHOLE] * 8
        + [ANY] * (1 + len(arrays)),
        out_specs=[WHOLE] * 3 + [ANY] * 2,
        scratch_shapes=[
            pltpu.VMEM((3, D, D), BF),
            pltpu.VMEM((D, D), BF),
            pltpu.VMEM((D, D), BF),
            pltpu.VMEM((D, FF), BF),
            pltpu.VMEM((FF, D), BF),
            pltpu.VMEM((rows, FF), F32),
            pltpu.VMEM((rows, FF), BF),
            pltpu.VMEM((rows, FF), BF),
            pltpu.VMEM((3, rows, D), BF),
            pltpu.VMEM((rows, D), BF),
            pltpu.VMEM((rows, D), BF),
            pltpu.VMEM((2, 4, ROWS_S, HALF), BF),
            pltpu.SemaphoreType.DMA((7 + CHUNKS,)),
            pltpu.SemaphoreType.DMA((2,)),
        ],
        out_shape=[
            sds((rows, D), F32),
            sds((rows, D), BF),
            sds((rows, 128), F32),
            sds((4, ROWS_S, HALF), BF),
            sds((4, ROWS_S, HALF), BF),
        ],
        compiler_params=PARAMS,
        cost_estimate=cost(50 * rows * D * D, 16 * D * D * 4),
        name="third_block",
    )(meta, g3, z2, z1, o2, qkv, o, l, gb, hidden, *arrays)


def attend_back_kernel(padded, q_ref, du_ref, dl_ref, mask_ref, k_ref, v_ref, dk_ref, dv_ref, dq_ref, dlt):
    pair = pl.program_id(1)

    @pl.when(pair == 0)
    def _():
        dlt[...] = dl_ref[0].T

    qbd = block_diag(q_ref[0])
    dubd = block_diag(du_ref[0])
    line = jnp.concatenate([dlt[pl.ds(2 * pair, 1), :], dlt[pl.ds(2 * pair + 1, 1), :]], 1)
    dqt = jnp.zeros((128, 2 * NLAT), F32)
    for first, width in spans(padded, 256):
        rows = slice(first, first + width)
        k, v = k_ref[0, rows, :], v_ref[0, rows, :]
        mask = mask_ref[0, rows, :]
        e = jnp.exp(nt(k, qbd) + jnp.concatenate([mask, mask], 1))
        ds = (e * (nt(v, dubd) + line)).astype(BF)
        dv_ref[0, rows, :] = nn(e.astype(BF), dubd).astype(BF)
        dk_ref[0, rows, :] = nn(ds, qbd).astype(BF)
        dqt = dqt + tn(k, ds)
    upper = lax.broadcasted_iota(jnp.int32, (128, NLAT), 0) < HEAD
    dq_ref[0] = (jnp.where(upper, dqt[:, :NLAT], dqt[:, NLAT:]).T * 0.125).astype(BF)


def attend_back(q, du, dl, mask, k, v):
    clips, padded = k.shape[0], k.shape[1]
    small = pl.BlockSpec((1, NLAT, 128), lambda i, j: (i, 0, j))
    whole = pl.BlockSpec((1, NLAT, 128), lambda i, j: (i, 0, 0))
    column = pl.BlockSpec((1, padded, 128), lambda i, j: (i, 0, 0))
    lanes = pl.BlockSpec((1, padded, 128), lambda i, j: (i, 0, j))
    return pl.pallas_call(
        functools.partial(attend_back_kernel, padded),
        grid=(clips, PAIRS),
        in_specs=[small, small, whole, column, lanes, lanes],
        out_specs=[lanes, lanes, small],
        scratch_shapes=[pltpu.VMEM((128, NLAT), F32)],
        out_shape=[sds((clips, padded, D), BF)] * 2 + [sds((clips, NLAT, D), BF)],
        compiler_params=PARAMS,
        cost_estimate=cost(
            20 * clips * padded * NLAT * D, clips * padded * D * 8, clips * padded * NLAT * HEADS
        ),
        name="attend_back",
    )(q, du, dl, mask, k, v)


def keyval_grad_kernel(meta, xl_ref, dk_ref, dv_ref, keep_ref, send_ref, sum_ref, acc, sums, shares, sems):
    f = meta[0]
    clip = pl.program_id(0)

    @pl.when(clip == 0)
    def _():
        acc[...] = jnp.zeros_like(acc)
        sums[...] = jnp.zeros_like(sums)

    xt = xl_ref[0].T
    for j, ref in enumerate((dk_ref, dv_ref)):
        for c in range(0, D, 256):
            acc[j, :, c : c + 256] += nn(xt, ref[0, :, c : c + 256])
        sums[j : j + 1, :] += column_sum(ref[0].astype(F32))

    @pl.when(clip == pl.num_programs(0) - 1)
    def _():
        for j in range(2):
            for g in range(OWNERS):
                rel = f ^ g
                grad = acc[j, g * SHARE : g * SHARE + SHARE, :].astype(BF)
                shares[rel & 1, rel >> 1, j * SHARE : j * SHARE + SHARE, :] = grad
        copies = []
        for which, ref in ((0, keep_ref), (1, send_ref)):
            for k in range(4):
                copies.append(
                    pltpu.make_async_copy(
                        shares.at[which, k], ref.at[k, pl.ds(0, 2 * SHARE)], sems.at[which, k]
                    )
                )
        for copy in copies:
            copy.start()
        sum_ref[...] = sums[...]
        for copy in copies:
            copy.wait()


def keyval_grad(meta, xl, dk, dv):
    clips, padded = xl.shape[0], xl.shape[1]
    block = pl.BlockSpec((1, padded, D), lambda i, m: (i, 0, 0))
    return pl.pallas_call(
        keyval_grad_kernel,
        grid_spec=pltpu.PrefetchScalarGridSpec(
            num_scalar_prefetch=1,
            grid=(clips,),
            in_specs=[block] * 3,
            out_specs=[ANY, ANY, pl.BlockSpec((8, D), lambda i, m: (0, 0))],
            scratch_shapes=[
                pltpu.VMEM((2, D, D), F32),
                pltpu.VMEM((8, D), F32),
                pltpu.VMEM((2, 4, 2 * SHARE, D), BF),
                pltpu.SemaphoreType.DMA((2, 4)),
            ],
        ),
        out_shape=[sds((4, ROWS_K, D), BF), sds((4, ROWS_K, D), BF), sds((8, D), F32)],
        compiler_params=PARAMS,
        cost_estimate=cost(4 * clips * padded * D * D, clips * padded * D * 6),
        name="keyval_grad",
    )(meta, xl, dk, dv)


def query_grad_kernel(pack, count, meta, *refs):
    own_ref, parts, refs = refs[0], refs[1:count], refs[count:]
    lat_ref, gb_ref, sum_ref, keep_in, send_in = refs[:5]
    refs = refs[5:]
    n_w = len(pack.arrays)
    wrefs, (back_ref, keep_ref, send_ref, wq, shares, sem, osems) = refs[:n_w], refs[n_w:]
    f = meta[0]
    start_square(pack, wrefs, 0, wq, f, sem.at[0])
    total = own_ref[...].astype(F32)
    for part in parts:
        total = total + part[...].astype(F32)
    dq = total.astype(BF)
    lat = lat_ref[...].astype(F32)
    zl = ln(lat, gb_ref[0:1], gb_ref[5:6]).astype(BF)
    grad = tn(zl, dq).astype(BF)
    for g in range(OWNERS):
        rel = f ^ g
        shares[rel & 1, rel >> 1, 0:SHARE, :] = grad[g * SHARE : g * SHARE + SHARE]
    wait_for(wq, sem.at[0])
    dzl = nt(dq, wq[...])
    back, dgain = ln_back(lat, gb_ref[0:1], dzl)
    back_ref[...] = back.astype(BF)
    lines = [sum_ref[0:1], sum_ref[1:2], column_sum(dgain), column_sum(dzl)]
    vec = jnp.concatenate(lines + [jnp.zeros((VEC_K - 4, D), F32)], 0).astype(BF)
    copies = []
    for which, ref in ((0, keep_ref), (1, send_ref)):
        for k in range(4):
            shares[which, k, SHARE : SHARE + VEC_K, :] = vec
            copies.append(
                pltpu.make_async_copy(
                    shares.at[which, k],
                    ref.at[k, pl.ds(2 * SHARE, SHARE + VEC_K)],
                    osems.at[which, k],
                )
            )
    for copy in copies:
        copy.start()
    for copy in copies:
        copy.wait()


def query_grad(pack, meta, dq, parts, lat, gb, sums, keep, send):
    rows = parts[0].shape[0] if parts else dq.shape[0]
    count = 1 + len(parts)
    mine = pl.BlockSpec((rows, D), lambda i, m: (m[1], 0))
    fixed = lambda shape: pl.BlockSpec(shape, lambda i, m: (0,) * len(shape))
    return pl.pallas_call(
        functools.partial(query_grad_kernel, pack, count),
        grid_spec=pltpu.PrefetchScalarGridSpec(
            num_scalar_prefetch=1,
            grid=(1,),
            in_specs=[mine]
            + [fixed((rows, D))] * len(parts)
            + [mine, fixed((16, D)), fixed((8, D)), ANY, ANY]
            + [ANY] * len(pack.arrays),
            out_specs=[fixed((rows, D)), ANY, ANY],
            scratch_shapes=[
                pltpu.VMEM((D, D), BF),
                pltpu.VMEM((2, 4, SHARE + VEC_K, D), BF),
                pltpu.SemaphoreType.DMA((1,)),
                pltpu.SemaphoreType.DMA((2, 4)),
            ],
        ),
        out_shape=[sds((rows, D), BF), sds(keep.shape, BF), sds(send.shape, BF)],
        input_output_aliases={count + 4: 1, count + 5: 2},
        compiler_params=PARAMS,
        name="query_grad",
    )(meta, dq, *parts, lat, gb, sums, keep, send, *pack.arrays)


def token_grad_kernel(pack, meta, x_ref, gb_ref, dk_ref, dv_ref, *refs):
    count = len(pack.arrays)
    wrefs, (out_ref, wkv, sems) = refs[:count], refs[count:]

    @pl.when((pl.program_id(0) == 0) & (pl.program_id(1) == 0))
    def _():
        f = meta[0]
        start_square(pack, wrefs, 0, wkv.at[0], f, sems.at[0])
        start_square(pack, wrefs, SHARE, wkv.at[1], f, sems.at[1])
        wait_for(wkv.at[0], sems.at[0])
        wait_for(wkv.at[1], sems.at[1])

    grad = nt(dk_ref[0], wkv[0]) + nt(dv_ref[0], wkv[1])
    back, unused = ln_back(x_ref[0].astype(F32), gb_ref[1:2], grad)
    out_ref[0] = back


def token_grad(pack, meta, tokens, gb, dk, dv):
    clips, local = tokens.shape[0], tokens.shape[1]
    padded = dk.shape[1]
    tile = padded // 4
    block = pl.BlockSpec((1, tile, D), lambda i, j, m: (i, j, 0))
    return pl.pallas_call(
        functools.partial(token_grad_kernel, pack),
        grid_spec=pltpu.PrefetchScalarGridSpec(
            num_scalar_prefetch=1,
            grid=(clips, padded // tile),
            in_specs=[block, pl.BlockSpec((16, D), lambda i, j, m: (0, 0)), block, block]
            + [ANY] * len(pack.arrays),
            out_specs=block,
            scratch_shapes=[pltpu.VMEM((2, D, D), BF), pltpu.SemaphoreType.DMA((2,))],
        ),
        out_shape=sds((clips, local, D), F32),
        compiler_params=PARAMS,
        cost_estimate=cost(4 * clips * padded * D * D, clips * padded * D * 10),
        name="token_grad",
    )(meta, tokens, gb, dk, dv, *pack.arrays)


def fold_kernel(keep_ref, recv_ref, *out_refs):
    for k, ref in enumerate(out_refs):
        ref[...] = (keep_ref[k].astype(F32) + recv_ref[k].astype(F32)).astype(BF)


def fold(keep, recv):
    shape = keep.shape[1:]
    lanes = 128
    block = pl.BlockSpec((4, shape[0], lanes), lambda i: (0, 0, i))
    return pl.pallas_call(
        fold_kernel,
        grid=(shape[1] // lanes,),
        in_specs=[block, block],
        out_specs=[pl.BlockSpec((shape[0], lanes), lambda i: (0, i))] * 4,
        out_shape=[sds(shape, BF)] * 4,
        compiler_params=PARAMS,
        name="fold",
    )(keep, recv)


def sum_kernel(*refs):
    total = refs[0][...].astype(F32)
    for ref in refs[1:-1]:
        total = total + ref[...].astype(F32)
    refs[-1][...] = total.astype(BF)


def sum_of(parts):
    shape = parts[0].shape
    block = pl.BlockSpec((shape[0], 128), lambda i: (0, i))
    return pl.pallas_call(
        sum_kernel,
        grid=(shape[1] // 128,),
        in_specs=[block] * len(parts),
        out_specs=block,
        out_shape=sds(shape, BF),
        compiler_params=PARAMS,
        name="sum_parts",
    )(*parts)


def exchange(x, bit):
    return lax.ppermute(x, "fsdp", [(i, i ^ bit) for i in range(OWNERS)])


def reduce_shares(keep, send, size):
    if size == OWNERS:
        mine, first, second, third = fold(keep, exchange(send, 1))
        return sum_of([mine, exchange(first, 2), exchange(second, 4), exchange(third, 6)])
    full = jnp.stack([keep, send], 1).reshape(OWNERS, *keep.shape[1:])
    return lax.psum(full.astype(F32), "fsdp").astype(BF)


def unpack(left_f, right_f, left_s, right_s, whole_k):
    sides_f, sides_s = (left_f, right_f), (left_s, right_s)
    span = CHUNKS * SHARE

    def up(sides):
        return jnp.concatenate(
            [x[c * SHARE : c * SHARE + SHARE] for x in sides for c in range(CHUNKS)], 1
        )

    def down(sides):
        return jnp.concatenate([x[span : 2 * span] for x in sides], 1)

    def square(i):
        at = 2 * span + i * SHARE
        return jnp.concatenate([x[at : at + SHARE] for x in sides_s], 1)

    q1, k1, v1, out1, out0 = (square(i) for i in range(5))
    k0, v0, q0 = (whole_k[i * SHARE : i * SHARE + SHARE] for i in range(3))
    return (
        jnp.stack([jnp.stack([q0, k0, v0]), jnp.stack([q1, k1, v1])]).astype(F32),
        jnp.stack([out0, out1]).astype(F32),
        jnp.stack([up(sides_s), up(sides_f)]).astype(F32),
        jnp.stack([down(sides_s), down(sides_f)]).astype(F32),
    )


def per_device(size, seq, *args):
    (
        latents_in,
        inputs,
        clip_frames,
        text_mask,
        qkv_weight,
        out_weight,
        mlp_in,
        mlp_out,
        norm_gain,
        norm_bias,
        bias_in,
        bias_out,
        out_cotangent,
    ) = args
    micro, clips, nlat, _ = latents_in.shape
    count = micro * clips
    local = inputs.shape[2]
    padded = -(-local // 128) * 128
    rows = count * nlat
    s = lax.axis_index("seq")
    fsdp = lax.axis_index("fsdp")
    special = size == OWNERS
    meta = jnp.stack([fsdp if special else jnp.int32(0), s, s % 2]).astype(jnp.int32)
    lat = latents_in.reshape(rows, D)
    tokens = inputs.reshape(count, local, D)
    g4 = out_cotangent.reshape(rows, D)

    place = s * local + jnp.arange(padded, dtype=jnp.int32)
    frames = clip_frames.reshape(count, 1) * PATCHES
    text = text_mask.reshape(count, -1) > 0
    text_len = text.shape[1]
    slots = FRAMES * PATCHES
    wide = jnp.pad(text, ((0, 0), (slots, padded)))
    text_here = lax.dynamic_slice_in_dim(wide, s * local, padded, 1)
    valid = jnp.where(place[None] < slots, place[None] < frames, text_here)
    valid = valid & (jnp.arange(padded)[None] < local)
    bias = jnp.where(valid, 0.0, -1e30).astype(F32)
    mask = jnp.broadcast_to(bias[:, :, None], (count, padded, 128))

    def packs_of(qkv, out, up, down, gain, shift, up_b, down_b):
        small = jnp.concatenate(
            [
                jnp.pad(jnp.concatenate([gain, shift, down_b], 0), ((0, 0), (0, 128 - SHARE))),
                up_b.reshape(6, 128),
                jnp.zeros((14, 128), BF),
            ],
            0,
        )
        small = jnp.concatenate([small[:16], small[16:]], 1)
        small = jnp.pad(small, ((0, 0), (0, D - 256)))
        slabs = lambda i: up[i].reshape(SHARE, CHUNKS, D).transpose(1, 0, 2).reshape(CHUNKS * SHARE, D)
        return (
            jnp.concatenate([qkv[0, 1], qkv[0, 2], small], 0),
            jnp.concatenate([qkv[0, 0], out[0]], 0),
            jnp.concatenate([slabs(0), down[0]], 0),
            jnp.concatenate([qkv[1].reshape(3 * SHARE, D), out[1], slabs(1), down[1]], 0),
        )

    weights = (qkv_weight, out_weight, mlp_in, mlp_out, norm_gain, norm_bias, bias_in, bias_out)
    axes = (2, 1, 1, 1, 1, 1, 1, 1)
    if special:
        raw = packs_of(*weights)

        def core_of(x):
            return exchange(x, 1)

        def direct(x):
            p = {0: x, 2: exchange(x, 2), 4: exchange(x, 4), 6: exchange(x, 6)}
            return Pack(
                [p[m] if m % 2 == 0 else core_of(p[m - 1]) for m in range(OWNERS)],
                lambda m, row: (m, None, row),
            )

        def relayed(x):
            half = x.shape[0] // 2
            p2, p4 = exchange(x, 2), exchange(x, 4)
            a6, b6 = exchange(p2[:half], 4), exchange(p4[half:], 2)
            arrays = [x, core_of(x), p2, core_of(p2), p4, core_of(p4), a6, core_of(a6), b6, core_of(b6)]

            def where(m, row):
                if m < 6:
                    return (m, None, row)
                return (m, None, row) if row < half else (m + 2, None, row - half)

            return Pack(arrays, where)

        g1a, g1b = direct(raw[0]), direct(raw[1])
        g2, g34 = relayed(raw[2]), relayed(raw[3])
    else:
        full = []
        for w, axis in zip(weights, axes):
            whole = lax.all_gather(w, "fsdp", axis=axis, tiled=True)
            shape = whole.shape
            parts = whole.reshape(*shape[:axis], OWNERS, shape[axis] // OWNERS, *shape[axis + 1 :])
            full.append(jnp.moveaxis(parts, axis, 0))
        raw = jax.vmap(packs_of)(*full)
        g1a, g1b, g2, g34 = [Pack([x], lambda m, row: (0, m, row)) for x in raw]

    def shift_to(x, k):
        return lax.ppermute(x, "seq", [(i, (i + k) % seq) for i in range(seq)])

    def scatter_rows(x):
        step = x.shape[0] // seq
        out = []
        for k in range(1, seq):
            piece = lax.dynamic_slice_in_dim(x, ((s + k) % seq) * step, step, 0)
            out.append(shift_to(piece, k))
        return out

    def gather_rows(x):
        return [x] + [shift_to(x, k) for k in range(1, seq)]

    xl, k, v, gb, bins = keyval(g1a, meta, tokens, local, padded)
    pay, q = attend(g1b, meta, lat, gb, bias[:, None, :], k, v)
    pay = pay.reshape(rows, PAY)
    share = combine(meta, pay, scatter_rows(pay))
    o, l, z1, z2, hidden = first_block(g1b, g2, meta, gather_rows(share), lat, gb, bins)
    out, g3, qkv2, o2, keep_f, send_f = second_block(g34, meta, z2, g4, gb, bins)

    g1, du, dl, keep_s, send_s = third_block(g2, g34, g1b, meta, g3, z2, z1, o2, qkv2, o, l, gb, hidden)
    cube = lambda x: x.reshape(count, nlat, x.shape[-1])
    dk, dv, dq = attend_back(cube(q), cube(du), cube(dl), mask, k, v)
    dq = dq.reshape(rows, D)
    dq_parts = scatter_rows(dq)
    keep_k, send_k, sums = keyval_grad(meta, xl, dk, dv)
    back, keep_k, send_k = query_grad(g1b, meta, dq, dq_parts, lat, gb, sums, keep_k, send_k)
    token_grads = token_grad(g1a, meta, tokens, gb, dk, dv)

    lat_grad = g1 + place_rows(gather_rows(back), s, seq)

    mine_f = reduce_shares(keep_f, send_f, size)
    mine_s = reduce_shares(keep_s, send_s, size)
    mine_k = reduce_shares(keep_k, send_k, size)
    pair = [(i, i ^ 1) for i in range(seq)]
    first = s % 2 == 0

    def both(mine):
        other = lax.ppermute(mine, "seq", pair)
        return jnp.where(first, mine, other), jnp.where(first, other, mine)

    if special:
        own = lax.dynamic_slice_in_dim(mine_k, s * (ROWS_K // seq), ROWS_K // seq, 0)
        pieces = gather_rows(sum_of([own] + scatter_rows(mine_k)))
        whole_k = place_rows(pieces, s, seq)
    else:
        whole_k = lax.psum(mine_k.astype(F32), "seq")
    shares = (*both(mine_f), *both(mine_s), whole_k)
    if special:
        grads = unpack(*shares)
        head = lambda x: x.astype(F32)
    else:
        wide = jax.vmap(unpack)(*shares)
        grads = []
        for x, w, axis in zip(wide, weights, axes):
            x = jnp.moveaxis(x, 0, axis)
            x = x.reshape(*x.shape[:axis], -1, *x.shape[axis + 2 :])
            grads.append(lax.dynamic_slice_in_dim(x, fsdp * w.shape[axis], w.shape[axis], axis))
        head = lambda x: x[0].astype(F32)
    vec_f = head(shares[0])[-VEC_F:].reshape(-1, D)
    vec_s = head(shares[2])[-VEC_S:].reshape(-1, D)
    vec_k = head(whole_k)[-VEC_K:]
    step = norm_gain.shape[1]
    k0, v0 = grads[0][0, 1], grads[0][0, 2]
    own_k, own_v = qkv_weight[0, 1].astype(F32), qkv_weight[0, 2].astype(F32)
    own_gain, own_shift = norm_gain[1].astype(F32), norm_bias[1].astype(F32)
    db1 = jnp.sum(own_k * vec_k[0] + own_v * vec_k[1], -1)
    dg1 = (jnp.sum(own_k * k0 + own_v * v0, -1) - own_shift * db1) / own_gain
    lines = jnp.stack([vec_k[2], vec_s[0], vec_s[7], vec_f[0], vec_k[3], vec_s[1], vec_s[8], vec_f[1], vec_s[2], vec_f[2]])
    cut = lax.dynamic_slice_in_dim(lines, fsdp * step, step, 1)
    wide_bias = jnp.stack([vec_s[3:7].reshape(FF), vec_f[3:7].reshape(FF)])
    return (
        out.reshape(latents_in.shape),
        lat_grad.reshape(latents_in.shape),
        token_grads.reshape(inputs.shape),
        *grads,
        jnp.stack([cut[0], dg1, cut[1], cut[2], cut[3]]),
        jnp.stack([cut[4], db1, cut[5], cut[6], cut[7]]),
        lax.dynamic_slice_in_dim(wide_bias, fsdp * bias_in.shape[1], bias_in.shape[1], 1),
        cut[8:10],
    )


def place_rows(pieces, s, seq):
    step = pieces[0].shape[0]
    whole = jnp.zeros((seq * step, *pieces[0].shape[1:]), F32)
    for k, piece in enumerate(pieces):
        at = ((s - k) % seq) * step
        whole = lax.dynamic_update_slice_in_dim(whole, piece.astype(F32), at, 0)
    return whole


def solution(mesh):
    in_specs = (
        P(None, "fsdp", None, None),
        P(None, "fsdp", "seq", None),
        P(None, "fsdp"),
        P(None, "fsdp", None),
        P(None, None, "fsdp", None),
        P(None, "fsdp", None),
        P(None, "fsdp", None),
        P(None, "fsdp", None),
        P(None, "fsdp"),
        P(None, "fsdp"),
        P(None, "fsdp"),
        P(None, "fsdp"),
        P(None, "fsdp", None, None),
    )
    out_specs = (
        P(None, "fsdp", None, None),
        P(None, "fsdp", None, None),
        P(None, "fsdp", "seq", None),
        P(None, None, "fsdp", None),
        P(None, "fsdp", None),
        P(None, "fsdp", None),
        P(None, "fsdp", None),
        P(None, "fsdp"),
        P(None, "fsdp"),
        P(None, "fsdp"),
        P(None, "fsdp"),
    )
    step = functools.partial(per_device, mesh.shape["fsdp"], mesh.shape["seq"])
    return jax.shard_map(step, mesh=mesh, in_specs=in_specs, out_specs=out_specs, check_vma=False)
```

time: 1280 us -> 507 us (0.40)
  waiting for transfers between devices: 544 us -> 165 us
  matrix products: 246 us -> 0 us
  Pallas kernels: 0 us -> 188 us
  local copies, waits for them, and re-layouts: 220 us -> 68.4 us
  blocking collectives: 148 us -> 0 us
  other arithmetic: 91.5 us -> 20.3 us
  starting transfers between devices: 2.18 us -> 54.2 us
  between operations: 20.5 us -> 2.07 us
    reduce_scatter x7 -> x0, waiting for transfers between devices: 309 us -> none  [the longest x1 130 us: per_device(): lax.psum_scatter(grad_sum[2], 'fsdp', scatter_dimension=1, tiled=True)]
    dot_general x78 -> x0, matrix products: 246 us -> none  [product(): return jnp.einsum(form, left, right, preferred_element_type=jnp.float32)]
    pallas_call x0 -> x17, Pallas kernels: none -> 188 us  [the longest x1 25.2 us: attend_back(): pl.pallas_call(functools.partial(attend_back_kernel, padded), grid=(clips...]
    ppermute x0 -> x64, waiting for transfers between devices: none -> 165 us  [the longest x44 95 us: exchange(): return lax.ppermute(x, 'fsdp', [(i, i ^ bit) for i in range(OWNERS)])]
    unnamed x22 -> x0, waiting for transfers between devices: 139 us -> none
    all_gather x10 -> x0, blocking collectives: 118 us -> none  [the longest x2 30.2 us: cross_forward(): lax.all_gather(numer_share, 'seq', axis=2, tiled=True)]
    all_gather x4 -> x0, waiting for transfers between devices: 68 us -> none  [the longest x1 52.4 us: per_device(): lax.all_gather(mlp_out, 'fsdp', axis=1, tiled=True)]
    ppermute x0 -> x64, starting transfers between devices: none -> 54.2 us  [the longest x44 32.7 us: exchange(): return lax.ppermute(x, 'fsdp', [(i, i ^ bit) for i in range(OWNERS)])]
  transfers between devices with their start and end apart: 17 -> 64, of which waited for: 8 -> 24; matrix products, arithmetic and copies ran while one was open for 27% -> 12% of each run, Pallas kernels for 0% -> 21%
where the time goes in v1:
time: 507 us; the launch traced here: 498 us
  Pallas kernels  188 us (37%)
  waiting for transfers between devices  165 us (33%)
  local copies, waits for them, and re-layouts  68.4 us (13%)
  starting transfers between devices  54.2 us (11%)
  other arithmetic  20.3 us (4%)
    ppermute x44, waiting for transfers between devices, exchange(): return lax.ppermute(x, 'fsdp', [(i, i ^ bit) for i in range(OWNERS)])  95 us
    ppermute x18, waiting for transfers between devices, shift_to(): return lax.ppermute(x, 'seq', [(i, (i + k) % seq) for i in range(seq)])  46.5 us
    unnamed x119, local copies, waits for them, and re-layouts  43.7 us
    ppermute x44, starting transfers between devices, exchange(): return lax.ppermute(x, 'fsdp', [(i, i ^ bit) for i in range(OWNERS)])  32.7 us
    pallas_call x1, Pallas kernels, attend_back(): pl.pallas_call(functools.partial(attend_back_kernel, padded), grid=(clips...  25.2 us
    pallas_call x1, Pallas kernels, third_block(): pl.pallas_call(functools.partial(third_kernel, ff_pack, self_pack, wo_pac...  24.9 us
    ppermute x2, waiting for transfers between devices, both(): other = lax.ppermute(mine, 'seq', pair)  23.6 us
    ppermute x18, starting transfers between devices, shift_to(): return lax.ppermute(x, 'seq', [(i, (i + k) % seq) for i in range(seq)])  20.9 us
  transfers between devices with their start and end apart: 64, of which 24 were waited for; matrix products, arithmetic and copies ran while one was open for 12% of the time, Pallas kernels for 21%

profile of v1, /device:TPU:0, one launch (start us, length us, event | category | flops | bytes accessed | tf_op | source)
XLA Modules:
  0.0 498.5 jit_solution(1336665802495459989)
XLA Ops:
  4.0 2.9 collective-permute-start.1
  13.6 15.2 %collective-permute-done.10.refs_4_.refs_11_.refs_33_.refs_13_ = bf16[192,768]{1,0:T(8,128)(2,1)S(1)} collective-permute-done((bf16[192,768]{1,0:T(8,128)(2,1)S(1)}, bf16[192,768]{1,0:T(8,128)(2,1)S(1)}, u32[]{:S(2)}, u32[]{:S(2)}) %collective-permute-start.10) | collective-permute-done | bytes 294944 | tf_op jit(solution)/shard_map/ppermute | solution.py:942
  30.8 2.3 slice_bitcast_fusion
  40.5 5.2 %copy.45 = bf16[2,1,1578,768]{3,2,0,1:T(8,128)(2,1)} copy(bf16[2,1,1578,768]{3,0,2,1:T(2,128)(2,1)} %param.14) | data formatting | bytes 9695232 | tf_op args[1]
  49.4 2.6 pad_maximum_fusion.refs_0_.refs_19_
  56.0 16.7 %keyval.1 = (bf16[2,1664,768]{2,1,0:T(8,128)(2,1)}, bf16[2,1664,768]{2,1,0:T(8,128)(2,1)}, bf16[2,1664,768]{2,1,0:T(8,128)(2,1)}, f32[16,768]{1,0:T(8,128)}, f32[2,3072]{1,0:T(2,128)}) custom-call(s32[3]{0:T(128)} %pad_add_fusion.meta.refs_0_, bf16[2,1578,768]{2,1,0:T(8,128)(2,1)} %bitcast.133, bf16[208,768]{1,0:T(8,128)(2,1)} %pad_maximum_fusion.3.refs_0_, ...), custom_call_target="tpu_custom_call" | custom-call | flops 7851737088 | bytes 20447232 | tf_op jit(solution)/shard_map/keyval/pallas_call | solution.py:205
  72.8 16.8 %attend.1 = (bf16[2,128,896]{2,1,0:T(8,128)(2,1)}, bf16[256,768]{1,0:T(8,128)(2,1)}) custom-call(s32[3]{0:T(128)} %pad_add_fusion.meta.refs_0_, bf16[256,768]{1,0:T(8,128)(2,1)} %bitcast.135, f32[16,768]{1,0:T(8,128)} %get-tuple-element.55.gb_ref.refs_5_.refs_7_, f32[2,1,1664]{2,1,0:T(1,128)} %broadcast_in_dim.38.bias_ref, ...), custom_call_target="tpu_custom_call" | custom-call | flops 2617245696 | bytes 10223616 | tf_op jit(solution)/shard_map/attend/pallas_call | solution.py:283
  96.2 2.0 collective-permute-done.14.refs_2_
  98.9 6.5 %collective-permute-done.15.refs_3_ = bf16[64,896]{1,0:T(8,128)(2,1)S(1)} collective-permute-done((bf16[64,896]{1,0:T(8,128)(2,1)S(1)}, bf16[64,896]{1,0:T(8,128)(2,1)S(1)}, u32[]{:S(2)}, u32[]{:S(2)}) %collective-permute-start.15) | collective-permute-done | bytes 114720 | tf_op jit(solution)/shard_map/ppermute | solution.py:1080
  105.4 2.5 collective-permute-start.16
  107.9 2.7 collective-permute-done.16.refs_4_
  110.6 2.6 combine.1.refs_0_
  113.2 7.3 %collective-permute-done.17.refs_1_ = bf16[64,896]{1,0:T(8,128)(2,1)S(1)} collective-permute-done((bf16[64,896]{1,0:T(8,128)(2,1)}, bf16[64,896]{1,0:T(8,128)(2,1)S(1)}, u32[]{:S(2)}, u32[]{:S(2)}) %collective-permute-start.17) | collective-permute-done | bytes 114720 | tf_op jit(solution)/shard_map/ppermute | solution.py:1080
  120.8 6.6 %collective-permute-done.18.refs_2_ = bf16[64,896]{1,0:T(8,128)(2,1)S(1)} collective-permute-done((bf16[64,896]{1,0:T(8,128)(2,1)}, bf16[64,896]{1,0:T(8,128)(2,1)S(1)}, u32[]{:S(2)}, u32[]{:S(2)}) %collective-permute-start.18) | collective-permute-done | bytes 114720 | tf_op jit(solution)/shard_map/ppermute | solution.py:1080
  127.4 1.9 collective-permute-start.19
  129.3 3.6 collective-permute-done.19.refs_3_
  139.8 2.7 collective-permute-done.24.refs_20_.refs_14_
  142.6 16.8 %collective-permute-done.34.refs_6_.refs_25_ = bf16[576,768]{1,0:T(8,128)(2,1)} collective-permute-done((bf16[576,768]{1,0:T(8,128)(2,1)S(1)}, bf16[576,768]{1,0:T(8,128)(2,1)}, u32[]{:S(2)}, u32[]{:S(2)}) %collective-permute-start.34) | collective-permute-done | bytes 884768 | tf_op jit(solution)/shard_map/ppermute | solution.py:942
  161.1 10.8 %first_block.1 = (bf16[256,768]{1,0:T(8,128)(2,1)}, f32[256,128]{1,0:T(8,128)}, f32[256,768]{1,0:T(8,128)}, f32[256,768]{1,0:T(8,128)}, f32[256,3072]{1,0:T(8,128)}) custom-call(s32[3]{0:T(128)} %pad_add_fusion.meta.refs_0_, bf16[64,896]{1,0:T(8,128)(2,1)} %combine.1.refs_0_, bf16[64,896]{1,0:T(8,128)(2,1)} %copy-done.32, bf16[64,896]{1,0:T(8,128)(2,1)} %copy-done.33, ...), custom_call_target="tpu_custom_call" | custom-call | flops 2717908992 | bytes 18874368 | tf_op jit(solution)/shard_map/first_block/pallas_call | solution.py:386
  173.8 19.3 %second_block.1 = (f32[256,768]{1,0:T(8,128)}, f32[256,768]{1,0:T(8,128)}, bf16[3,256,768]{2,1,0:T(8,128)(2,1)}, bf16[256,768]{1,0:T(8,128)(2,1)}, bf16[4,784,38...) custom-call(s32[3]{0:T(128)} %pad_add_fusion.meta.refs_0_, f32[256,768]{1,0:T(8,128)} %get-tuple-element.60.z2_ref.refs_1_, ...), custom_call_target="tpu_custom_call" | custom-call | flops 7549747200 | bytes 28311552 | tf_op jit(solution)/shard_map/second_block/pallas_call | solution.py:523
  193.1 24.9 %third_block.1 = (f32[256,768]{1,0:T(8,128)}, bf16[256,768]{1,0:T(8,128)(2,1)}, f32[256,128]{1,0:T(8,128)}, bf16[4,1280,384]{2,1,0:T(8,128)(2,1)}, bf16[4,1280,384]{2,1,0:T(8,128)(2,1)}) custom-call(s32[3]{0:T(128)} %pad_add_fusion.meta.refs_0_, f32[256,768]{1,0:T(8,128)} %get-tuple-element.62.refs_0_, f32[256,768]{1,0:T(8,128)} %get-tuple-element.60.z2_ref.refs_1_, ...), custom_call_target="tpu_custom_call" | custom-call | flops 7549747200 | bytes 37748736 | tf_op jit(solution)/shard_map/third_block/pallas_call | solution.py:650
  219.7 25.2 %attend_back.1 = (bf16[2,1664,768]{2,1,0:T(8,128)(2,1)}, bf16[2,1664,768]{2,1,0:T(8,128)(2,1)}, bf16[2,128,768]{2,1,0:T(8,128)(2,1)}) custom-call(bf16[2,128,768]{2,1,0:T(8,128)(2,1)} %bitcast.161, bf16[2,128,768]{2,1,0:T(8,128)(2,1)} %bitcast.162, f32[2,128,128]{2,1,0:T(8,128)} %bitcast.163, f32[2,1664,128]{2,1,0:T(8,128)} %broadcast_in_dim.40.mask_ref, ...), custom_call_target="tpu_custom_call" | custom-call | flops 6543114240 | bytes 20447232 | tf_op jit(solution)/shard_map/attend_back/pallas_call | solution.py:715
  247.0 2.9 collective-permute-start.39
  250.1 16.1 %keyval_grad.1 = (bf16[4,320,768]{2,1,0:T(8,128)(2,1)}, bf16[4,320,768]{2,1,0:T(8,128)(2,1)}, f32[8,768]{1,0:T(8,128)}) custom-call(s32[3]{0:T(128)} %pad_add_fusion.meta.refs_0_, bf16[2,1664,768]{2,1,0:T(8,128)(2,1)} %get-tuple-element.74.xl_ref, bf16[2,1664,768]{2,1,0:T(8,128)(2,1)} %get-tuple-element.75.dk_ref, bf16[2,1664,768]{2,1,0:T(8,128)(2,1)} %get-tuple-element.76.dv_ref), custom_call_target="tpu_custom_call" | custom-call | flops 7851737088 | bytes 15335424 | tf_op jit(solution)/shard_map/keyval_grad/pallas_call | solution.py:770
  266.9 6.3 %query_grad.1 = (bf16[64,768]{1,0:T(8,128)(2,1)}, bf16[4,320,768]{2,1,0:T(8,128)(2,1)}, bf16[4,320,768]{2,1,0:T(8,128)(2,1)}) custom-call(s32[3]{0:T(128)} %pad_add_fusion.meta.refs_0_, bf16[256,768]{1,0:T(8,128)(2,1)} %bitcast.144, bf16[64,768]{1,0:T(8,128)(2,1)} %copy-done.36, ...), custom_call_target="tpu_custom_call", output_to_operand_aliasing={{1}: (8, {}), {2}: (9, {})} | custom-call | tf_op jit(solution)/shard_map/query_grad/pallas_call | solution.py:837
  273.8 2.0 collective-permute-start.41
  275.9 18.3 %token_grad.1 = f32[2,1578,768]{2,1,0:T(8,128)} custom-call(s32[3]{0:T(128)} %pad_add_fusion.meta.refs_0_, bf16[2,1578,768]{2,1,0:T(8,128)(2,1)} %bitcast.134, f32[16,768]{1,0:T(8,128)} %get-tuple-element.55.gb_ref.refs_5_.refs_7_, bf16[2,1664,768]{2,1,0:T(8,128)(2,1)} %get-tuple-element.75.dk_ref, bf16[2,1664,768]{2,1,0:T(8,128)(2,1)} %get-tuple-element.76.dv_ref, ...), custom_call_target="tpu_custom_call" | custom-call | flops 7851737088 | bytes 25559040 | tf_op jit(solution)/shard_map/token_grad/pallas_call | solution.py:883
  294.2 24.6 %copy.31 = f32[2,1,1578,768]{3,1,2,0:T(1,128)} copy(f32[2,1,1578,768]{3,2,0,1:T(8,128)} %bitcast.132) | data formatting | bytes 19390464
  318.9 5.1 %fold.3 = (bf16[320,768]{1,0:T(8,128)(2,1)}, bf16[320,768]{1,0:T(8,128)(2,1)}, bf16[320,768]{1,0:T(8,128)(2,1)}, bf16[320,768]{1,0:T(8,128)(2,1)}) custom-call(bf16[4,320,768]{2,1,0:T(8,128)(2,1)} %get-tuple-element.81.keep_ref, bf16[4,320,768]{2,1,0:T(8,128)(2,1)} %collective-permute-done.44.recv_ref), custom_call_target="tpu_custom_call" | custom-call | tf_op jit(solution)/shard_map/fold/pallas_call | solution.py:909
  328.5 9.8 %collective-permute-done.45.refs_1_ = bf16[320,768]{1,0:T(8,128)(2,1)S(1)} collective-permute-done((bf16[320,768]{1,0:T(8,128)(2,1)}, bf16[320,768]{1,0:T(8,128)(2,1)S(1)}, u32[]{:S(2)}, u32[]{:S(2)}) %collective-permute-start.45) | collective-permute-done | bytes 491552 | tf_op jit(solution)/shard_map/ppermute | solution.py:942
  338.3 2.8 collective-permute-start.43
  341.1 8.1 %collective-permute-done.46.refs_2_ = bf16[320,768]{1,0:T(8,128)(2,1)S(1)} collective-permute-done((bf16[320,768]{1,0:T(8,128)(2,1)}, bf16[320,768]{1,0:T(8,128)(2,1)S(1)}, u32[]{:S(2)}, u32[]{:S(2)}) %collective-permute-start.46) | collective-permute-done | bytes 491552 | tf_op jit(solution)/shard_map/ppermute | solution.py:942
  350.8 4.6 sum_parts.4
  355.4 1.9 constant_dynamic-slice_fusion.1
  357.3 2.0 collective-permute-start.48
  359.3 2.4 collective-permute-start.50
  365.1 4.6 fold.5
  373.1 3.6 sum_parts.5
  377.8 6.7 %collective-permute-done.51 = bf16[80,768]{1,0:T(8,128)(2,1)S(1)} collective-permute-done((bf16[80,768]{1,0:T(8,128)(2,1)}, bf16[80,768]{1,0:T(8,128)(2,1)S(1)}, u32[]{:S(2)}, u32[]{:S(2)}) %collective-permute-start.51) | collective-permute-done | bytes 122912 | tf_op jit(solution)/shard_map/ppermute | solution.py:1080
  384.5 6.1 %collective-permute-done.52 = bf16[80,768]{1,0:T(8,128)(2,1)S(1)} collective-permute-done((bf16[80,768]{1,0:T(8,128)(2,1)}, bf16[80,768]{1,0:T(8,128)(2,1)S(1)}, u32[]{:S(2)}, u32[]{:S(2)}) %collective-permute-start.52) | collective-permute-done | bytes 122912 | tf_op jit(solution)/shard_map/ppermute | solution.py:1080
  390.9 5.0 %collective-permute-done.53 = bf16[80,768]{1,0:T(8,128)(2,1)S(1)} collective-permute-done((bf16[80,768]{1,0:T(8,128)(2,1)}, bf16[80,768]{1,0:T(8,128)(2,1)S(1)}, u32[]{:S(2)}, u32[]{:S(2)}) %collective-permute-start.53) | collective-permute-done | bytes 122912 | tf_op jit(solution)/shard_map/ppermute | solution.py:1080
  397.6 3.4 sum_parts.7
  403.6 8.3 %collective-permute-done.63 = bf16[784,384]{1,0:T(8,128)(2,1)S(1)} collective-permute-done((bf16[784,384]{1,0:T(8,128)(2,1)}, bf16[784,384]{1,0:T(8,128)(2,1)S(1)}, u32[]{:S(2)}, u32[]{:S(2)}) %collective-permute-start.63) | collective-permute-done | bytes 602144 | tf_op jit(solution)/shard_map/ppermute | solution.py:1118
  412.1 6.0 %fold.4 = (bf16[1280,384]{1,0:T(8,128)(2,1)}, bf16[1280,384]{1,0:T(8,128)(2,1)}, bf16[1280,384]{1,0:T(8,128)(2,1)}, bf16[1280,384]{1,0:T(8,128)(2,1)}) custom-call(bf16[4,1280,384]{2,1,0:T(8,128)(2,1)} %get-tuple-element.87.keep_ref, bf16[4,1280,384]{2,1,0:T(8,128)(2,1)} %collective-permute-done.54.recv_ref), custom_call_target="tpu_custom_call" | custom-call | tf_op jit(solution)/shard_map/fold/pallas_call | solution.py:909
  423.2 20.0 %collective-permute-done.55.refs_1_ = bf16[1280,384]{1,0:T(8,128)(2,1)} collective-permute-done((bf16[1280,384]{1,0:T(8,128)(2,1)}, bf16[1280,384]{1,0:T(8,128)(2,1)}, u32[]{:S(2)}, u32[]{:S(2)}) %collective-permute-start.55) | collective-permute-done | bytes 983072 | tf_op jit(solution)/shard_map/ppermute | solution.py:942
  443.2 15.7 %collective-permute-done.56.refs_2_ = bf16[1280,384]{1,0:T(8,128)(2,1)} collective-permute-done((bf16[1280,384]{1,0:T(8,128)(2,1)}, bf16[1280,384]{1,0:T(8,128)(2,1)}, u32[]{:S(2)}, u32[]{:S(2)}) %collective-permute-start.56) | collective-permute-done | bytes 983072 | tf_op jit(solution)/shard_map/ppermute | solution.py:942
  460.7 3.9 sum_parts.6
  467.9 15.3 %collective-permute-done.58 = bf16[1280,384]{1,0:T(8,128)(2,1)S(1)} collective-permute-done((bf16[1280,384]{1,0:T(8,128)(2,1)}, bf16[1280,384]{1,0:T(8,128)(2,1)S(1)}, u32[]{:S(2)}, u32[]{:S(2)}) %collective-permute-start.58) | collective-permute-done | bytes 983072 | tf_op jit(solution)/shard_map/ppermute | solution.py:1118
  (291 shorter events, 93.6 us)
Async XLA Ops:
  4.0 31.8 %collective-permute-start.1 = (bf16[208,768]{1,0:T(8,128)(2,1)}, bf16[208,768]{1,0:T(8,128)(2,1)}, u32[]{:S(2)}, u32[]{:S(2)}) collective-permute-start(bf16[208,768]{1,0:T(8,128)(2,1)} %pad_maximum_fusion.3.refs_0_), channel_id=1, source_target_pairs={{0,8},{4,12},{8,0},{12,4},{16,24},{20,28},{24,16},{28,20},{1,9},{5... | collective-permute-start | bytes 958472 | tf_op jit(solution)/shard_map/ppermute | solution.py:942
  6.9 29.0 %collective-permute-start.3 = (bf16[208,768]{1,0:T(8,128)(2,1)}, bf16[208,768]{1,0:T(8,128)(2,1)}, u32[]{:S(2)}, u32[]{:S(2)}) collective-permute-start(bf16[208,768]{1,0:T(8,128)(2,1)} %pad_maximum_fusion.3.refs_0_), channel_id=1, source_target_pairs={{0,16},{4,20},{8,24},{12,28},{16,0},{20,4},{24,8},{28,12},{1,17},{... | collective-permute-start | bytes 958472 | tf_op jit(solution)/shard_map/ppermute | solution.py:942
  8.5 20.3 %collective-permute-start.10 = (bf16[192,768]{1,0:T(8,128)(2,1)S(1)}, bf16[192,768]{1,0:T(8,128)(2,1)S(1)}, u32[]{:S(2)}, u32[]{:S(2)}) collective-permute-start(bf16[192,768]{1,0:T(8,128)(2,1)S(1)} %pad_maximum_fusion.4.refs_0_.refs_7_.refs_29_.refs_9_), channel_id=1, source_target_pairs={{0,16},{4,20},{8,24},{12,28},{16,0},{20,4},{24,8},{28,12},{1,17},{... | collective-permute-start | bytes 884744 | tf_op jit(solution)/shard_map/ppermute | solution.py:942
  9.1 21.2 %collective-permute-start.12 = (bf16[192,768]{1,0:T(8,128)(2,1)S(1)}, bf16[192,768]{1,0:T(8,128)(2,1)S(1)}, u32[]{:S(2)}, u32[]{:S(2)}) collective-permute-start(bf16[192,768]{1,0:T(8,128)(2,1)S(1)} %pad_maximum_fusion.4.refs_0_.refs_7_.refs_29_.refs_9_), channel_id=1, source_target_pairs={{0,24},{4,28},{8,16},{12,20},{16,8},{20,12},{24,0},{28,4},{1,25},{... | collective-permute-start | bytes 884744 | tf_op jit(solution)/shard_map/ppermute | solution.py:942
  10.6 19.7 %collective-permute-start.8 = (bf16[192,768]{1,0:T(8,128)(2,1)S(1)}, bf16[192,768]{1,0:T(8,128)(2,1)S(1)}, u32[]{:S(2)}, u32[]{:S(2)}) collective-permute-start(bf16[192,768]{1,0:T(8,128)(2,1)S(1)} %pad_maximum_fusion.4.refs_0_.refs_7_.refs_29_.refs_9_), channel_id=1, source_target_pairs={{0,8},{4,12},{8,0},{12,4},{16,24},{20,28},{24,16},{28,20},{1,9},{5... | collective-permute-start | bytes 884744 | tf_op jit(solution)/shard_map/ppermute | solution.py:942
  28.8 9.3 %collective-permute-start.5 = (bf16[208,768]{1,0:T(8,128)(2,1)}, bf16[208,768]{1,0:T(8,128)(2,1)}, u32[]{:S(2)}, u32[]{:S(2)}) collective-permute-start(bf16[208,768]{1,0:T(8,128)(2,1)} %pad_maximum_fusion.3.refs_0_), channel_id=1, source_target_pairs={{0,24},{4,28},{8,16},{12,20},{16,8},{20,12},{24,0},{28,4},{1,25},{... | collective-permute-start | bytes 958472 | tf_op jit(solution)/shard_map/ppermute | solution.py:942
  30.3 19.0 %collective-permute-start = (bf16[208,768]{1,0:T(8,128)(2,1)}, bf16[208,768]{1,0:T(8,128)(2,1)}, u32[]{:S(2)}, u32[]{:S(2)}) collective-permute-start(bf16[208,768]{1,0:T(8,128)(2,1)} %pad_maximum_fusion.3.refs_0_), channel_id=1, source_target_pairs={{0,4},{4,0},{8,12},{12,8},{16,20},{20,16},{24,28},{28,24},{1,5},{5... | collective-permute-start | bytes 958472 | tf_op jit(solution)/shard_map/ppermute | solution.py:942
  30.3 18.4 %collective-permute-start.7 = (bf16[192,768]{1,0:T(8,128)(2,1)S(1)}, bf16[192,768]{1,0:T(8,128)(2,1)S(1)}, u32[]{:S(2)}, u32[]{:S(2)}) collective-permute-start(bf16[192,768]{1,0:T(8,128)(2,1)S(1)} %pad_maximum_fusion.4.refs_0_.refs_7_.refs_29_.refs_9_), channel_id=1, source_target_pairs={{0,4},{4,0},{8,12},{12,8},{16,20},{20,16},{24,28},{28,24},{1,5},{5... | collective-permute-start | bytes 884744 | tf_op jit(solution)/shard_map/ppermute | solution.py:942
  35.8 18.2 %collective-permute-start.2 = (bf16[208,768]{1,0:T(8,128)(2,1)}, bf16[208,768]{1,0:T(8,128)(2,1)}, u32[]{:S(2)}, u32[]{:S(2)}) collective-permute-start(bf16[208,768]{1,0:T(8,128)(2,1)} %collective-permute-done.1.refs_2_), channel_id=1, source_target_pairs={{0,4},{4,0},{8,12},{12,8},{16,20},{20,16},{24,28},{28,24},{1,5},{5... | collective-permute-start | bytes 958472 | tf_op jit(solution)/shard_map/ppermute | solution.py:942
  36.0 19.5 %collective-permute-start.4 = (bf16[208,768]{1,0:T(8,128)(2,1)}, bf16[208,768]{1,0:T(8,128)(2,1)}, u32[]{:S(2)}, u32[]{:S(2)}) collective-permute-start(bf16[208,768]{1,0:T(8,128)(2,1)} %collective-permute-done.3.refs_4_), channel_id=1, source_target_pairs={{0,4},{4,0},{8,12},{12,8},{16,20},{20,16},{24,28},{28,24},{1,5},{5... | collective-permute-start | bytes 958472 | tf_op jit(solution)/shard_map/ppermute | solution.py:942
  38.1 17.9 %collective-permute-start.6 = (bf16[208,768]{1,0:T(8,128)(2,1)}, bf16[208,768]{1,0:T(8,128)(2,1)}, u32[]{:S(2)}, u32[]{:S(2)}) collective-permute-start(bf16[208,768]{1,0:T(8,128)(2,1)} %collective-permute-done.5.refs_6_), channel_id=1, source_target_pairs={{0,4},{4,0},{8,12},{12,8},{16,20},{20,16},{24,28},{28,24},{1,5},{5... | collective-permute-start | bytes 958472 | tf_op jit(solution)/shard_map/ppermute | solution.py:942
  51.9 40.3 %collective-permute-start.21 = (bf16[768,768]{1,0:T(8,128)(2,1)S(1)}, bf16[768,768]{1,0:T(8,128)(2,1)S(1)}, u32[]{:S(2)}, u32[]{:S(2)}) collective-permute-start(bf16[768,768]{1,0:T(8,128)(2,1)S(1)} %pad_maximum_fusion.2.refs_15_.refs_9_), channel_id=1, source_target_pairs={{0,8},{4,12},{8,0},{12,4},{16,24},{20,28},{24,16},{28,20},{1,9},{5... | collective-permute-start | bytes 3538952 | tf_op jit(solution)/shard_map/ppermute | solution.py:942
  52.6 42.1 %collective-permute-start.23 = (bf16[768,768]{1,0:T(8,128)(2,1)S(1)}, bf16[768,768]{1,0:T(8,128)(2,1)S(1)}, u32[]{:S(2)}, u32[]{:S(2)}) collective-permute-start(bf16[768,768]{1,0:T(8,128)(2,1)S(1)} %pad_maximum_fusion.2.refs_15_.refs_9_), channel_id=1, source_target_pairs={{0,16},{4,20},{8,24},{12,28},{16,0},{20,4},{24,8},{28,12},{1,17},{... | collective-permute-start | bytes 3538952 | tf_op jit(solution)/shard_map/ppermute | solution.py:942
  54.0 79.5 %collective-permute-start.30 = (bf16[1152,768]{1,0:T(8,128)(2,1)}, bf16[1152,768]{1,0:T(8,128)(2,1)}, u32[]{:S(2)}, u32[]{:S(2)}) collective-permute-start(bf16[1152,768]{1,0:T(8,128)(2,1)} %pad_maximum_fusion.refs_0_.refs_19_), channel_id=1, source_target_pairs={{0,8},{4,12},{8,0},{12,4},{16,24},{20,28},{24,16},{28,20},{1,9},{5... | collective-permute-start | bytes 5308424 | tf_op jit(solution)/shard_map/ppermute | solution.py:942
  55.5 78.4 %collective-permute-start.32 = (bf16[1152,768]{1,0:T(8,128)(2,1)}, bf16[1152,768]{1,0:T(8,128)(2,1)}, u32[]{:S(2)}, u32[]{:S(2)}) collective-permute-start(bf16[1152,768]{1,0:T(8,128)(2,1)} %pad_maximum_fusion.refs_0_.refs_19_), channel_id=1, source_target_pairs={{0,16},{4,20},{8,24},{12,28},{16,0},{20,4},{24,8},{28,12},{1,17},{... | collective-permute-start | bytes 5308424 | tf_op jit(solution)/shard_map/ppermute | solution.py:942
  56.0 16.7 %collective-permute-start.9 = (bf16[192,768]{1,0:T(8,128)(2,1)S(1)}, bf16[192,768]{1,0:T(8,128)(2,1)}, u32[]{:S(2)}, u32[]{:S(2)}) collective-permute-start(bf16[192,768]{1,0:T(8,128)(2,1)S(1)} %copy-done.7), channel_id=1, source_target_pairs={{0,4},{4,0},{8,12},{12,8},{16,20},{20,16},{24,28},{28,24},{1,5},{5... | collective-permute-start | bytes 884744 | tf_op jit(solution)/shard_map/ppermute | solution.py:942
  93.2 39.7 %collective-permute-start.25 = (bf16[384,768]{1,0:T(8,128)(2,1)}, bf16[384,768]{1,0:T(8,128)(2,1)}, u32[]{:S(2)}, u32[]{:S(2)}) collective-permute-start(bf16[384,768]{1,0:T(8,128)(2,1)} %slice.349), channel_id=1, source_target_pairs={{0,16},{4,20},{8,24},{12,28},{16,0},{20,4},{24,8},{28,12},{1,17},{... | collective-permute-start | bytes 1769480 | tf_op jit(solution)/shard_map/ppermute | solution.py:942
  95.6 37.8 %collective-permute-start.27 = (bf16[384,768]{1,0:T(8,128)(2,1)}, bf16[384,768]{1,0:T(8,128)(2,1)}, u32[]{:S(2)}, u32[]{:S(2)}) collective-permute-start(bf16[384,768]{1,0:T(8,128)(2,1)} %slice.350), channel_id=1, source_target_pairs={{0,8},{4,12},{8,0},{12,4},{16,24},{20,28},{24,16},{28,20},{1,9},{5... | collective-permute-start | bytes 1769480 | tf_op jit(solution)/shard_map/ppermute | solution.py:942
  136.6 35.4 %collective-permute-start.29 = (bf16[1152,768]{1,0:T(8,128)(2,1)}, bf16[1152,768]{1,0:T(8,128)(2,1)}, u32[]{:S(2)}, u32[]{:S(2)}) collective-permute-start(bf16[1152,768]{1,0:T(8,128)(2,1)} %pad_maximum_fusion.refs_0_.refs_19_), channel_id=1, source_target_pairs={{0,4},{4,0},{8,12},{12,8},{16,20},{20,16},{24,28},{28,24},{1,5},{5... | collective-permute-start | bytes 5308424 | tf_op jit(solution)/shard_map/ppermute | solution.py:942
  137.6 21.8 %collective-permute-start.34 = (bf16[576,768]{1,0:T(8,128)(2,1)S(1)}, bf16[576,768]{1,0:T(8,128)(2,1)}, u32[]{:S(2)}, u32[]{:S(2)}) collective-permute-start(bf16[576,768]{1,0:T(8,128)(2,1)S(1)} %slice.351), channel_id=1, source_target_pairs={{0,16},{4,20},{8,24},{12,28},{16,0},{20,4},{24,8},{28,12},{1,17},{... | collective-permute-start | bytes 2654216 | tf_op jit(solution)/shard_map/ppermute | solution.py:942
  139.3 21.8 %collective-permute-start.36 = (bf16[576,768]{1,0:T(8,128)(2,1)S(1)}, bf16[576,768]{1,0:T(8,128)(2,1)}, u32[]{:S(2)}, u32[]{:S(2)}) collective-permute-start(bf16[576,768]{1,0:T(8,128)(2,1)S(1)} %slice.352), channel_id=1, source_target_pairs={{0,8},{4,12},{8,0},{12,4},{16,24},{20,28},{24,16},{28,20},{1,9},{5... | collective-permute-start | bytes 2654216 | tf_op jit(solution)/shard_map/ppermute | solution.py:942
  139.8 32.2 %collective-permute-start.31 = (bf16[1152,768]{1,0:T(8,128)(2,1)}, bf16[1152,768]{1,0:T(8,128)(2,1)S(1)}, u32[]{:S(2)}, u32[]{:S(2)}) collective-permute-start(bf16[1152,768]{1,0:T(8,128)(2,1)} %collective-permute-done.30.refs_2_.refs_21_), channel_id=1, source_target_pairs={{0,4},{4,0},{8,12},{12,8},{16,20},{20,16},{24,28},{28,24},{1,5},{5... | collective-permute-start | bytes 5308424 | tf_op jit(solution)/shard_map/ppermute | solution.py:942
  142.5 29.5 %collective-permute-start.33 = (bf16[1152,768]{1,0:T(8,128)(2,1)}, bf16[1152,768]{1,0:T(8,128)(2,1)S(1)}, u32[]{:S(2)}, u32[]{:S(2)}) collective-permute-start(bf16[1152,768]{1,0:T(8,128)(2,1)} %collective-permute-done.32.refs_4_.refs_23_), channel_id=1, source_target_pairs={{0,4},{4,0},{8,12},{12,8},{16,20},{20,16},{24,28},{28,24},{1,5},{5... | collective-permute-start | bytes 5308424 | tf_op jit(solution)/shard_map/ppermute | solution.py:942
  159.4 12.5 %collective-permute-start.35 = (bf16[576,768]{1,0:T(8,128)(2,1)}, bf16[576,768]{1,0:T(8,128)(2,1)}, u32[]{:S(2)}, u32[]{:S(2)}) collective-permute-start(bf16[576,768]{1,0:T(8,128)(2,1)} %collective-permute-done.34.refs_6_.refs_25_), channel_id=1, source_target_pairs={{0,4},{4,0},{8,12},{12,8},{16,20},{20,16},{24,28},{28,24},{1,5},{5... | collective-permute-start | bytes 2654216 | tf_op jit(solution)/shard_map/ppermute | solution.py:942
  161.1 10.9 %collective-permute-start.37 = (bf16[576,768]{1,0:T(8,128)(2,1)}, bf16[576,768]{1,0:T(8,128)(2,1)}, u32[]{:S(2)}, u32[]{:S(2)}) collective-permute-start(bf16[576,768]{1,0:T(8,128)(2,1)} %collective-permute-done.36.refs_8_.refs_27_), channel_id=1, source_target_pairs={{0,4},{4,0},{8,12},{12,8},{16,20},{20,16},{24,28},{28,24},{1,5},{5... | collective-permute-start | bytes 2654216 | tf_op jit(solution)/shard_map/ppermute | solution.py:942
  245.9 20.3 %collective-permute-start.38 = (bf16[64,768]{1,0:T(8,128)(2,1)S(1)}, bf16[64,768]{1,0:T(8,128)(2,1)S(1)}, u32[]{:S(2)}, u32[]{:S(2)}) collective-permute-start(bf16[64,768]{1,0:T(8,128)(2,1)S(1)} %get-tuple-element.161), channel_id=1, source_target_pairs={{0,1},{1,2},{2,3},{3,0},{4,5},{5,6},{6,7},{7,4},{8,9},{9,10},{10,1... | collective-permute-start | bytes 294920 | tf_op jit(solution)/shard_map/ppermute | solution.py:1080
  247.0 19.3 %collective-permute-start.39 = (bf16[64,768]{1,0:T(8,128)(2,1)S(1)}, bf16[64,768]{1,0:T(8,128)(2,1)S(1)}, u32[]{:S(2)}, u32[]{:S(2)}) collective-permute-start(bf16[64,768]{1,0:T(8,128)(2,1)S(1)} %get-tuple-element.160), channel_id=1, source_target_pairs={{0,2},{1,3},{2,0},{3,1},{4,6},{5,7},{6,4},{7,5},{8,10},{9,11},{10,... | collective-permute-start | bytes 294920 | tf_op jit(solution)/shard_map/ppermute | solution.py:1080
  249.8 16.4 %collective-permute-start.40 = (bf16[64,768]{1,0:T(8,128)(2,1)S(1)}, bf16[64,768]{1,0:T(8,128)(2,1)S(1)}, u32[]{:S(2)}, u32[]{:S(2)}) collective-permute-start(bf16[64,768]{1,0:T(8,128)(2,1)S(1)} %get-tuple-element.159), channel_id=1, source_target_pairs={{0,3},{1,0},{2,1},{3,2},{4,7},{5,4},{6,5},{7,6},{8,11},{9,8},{10,9... | collective-permute-start | bytes 294920 | tf_op jit(solution)/shard_map/ppermute | solution.py:1080
  273.2 45.7 %collective-permute-start.44 = (bf16[4,320,768]{2,1,0:T(8,128)(2,1)}, bf16[4,320,768]{2,1,0:T(8,128)(2,1)}, u32[]{:S(2)}, u32[]{:S(2)}) collective-permute-start(bf16[4,320,768]{2,1,0:T(8,128)(2,1)} %get-tuple-element.82), channel_id=1, source_target_pairs={{0,4},{4,0},{8,12},{12,8},{16,20},{20,16},{24,28},{28,24},{1,5},{5... | collective-permute-start | bytes 5898248 | tf_op jit(solution)/shard_map/ppermute | solution.py:942
  273.3 90.4 %collective-permute-start.59 = (bf16[4,784,384]{2,1,0:T(8,128)(2,1)}, bf16[4,784,384]{2,1,0:T(8,128)(2,1)S(1)}, u32[]{:S(2)}, u32[]{:S(2)}) collective-permute-start(bf16[4,784,384]{2,1,0:T(8,128)(2,1)} %get-tuple-element.94), channel_id=1, source_target_pairs={{0,4},{4,0},{8,12},{12,8},{16,20},{20,16},{24,28},{28,24},{1,5},{5... | collective-permute-start | bytes 7225352 | tf_op jit(solution)/shard_map/ppermute | solution.py:942
  273.8 138.4 %collective-permute-start.54 = (bf16[4,1280,384]{2,1,0:T(8,128)(2,1)}, bf16[4,1280,384]{2,1,0:T(8,128)(2,1)}, u32[]{:S(2)}, u32[]{:S(2)}) collective-permute-start(bf16[4,1280,384]{2,1,0:T(8,128)(2,1)} %get-tuple-element.88), channel_id=1, source_target_pairs={{0,4},{4,0},{8,12},{12,8},{16,20},{20,16},{24,28},{28,24},{1,5},{5... | collective-permute-start | bytes 11796488 | tf_op jit(solution)/shard_map/ppermute | solution.py:942
  273.8 51.9 %collective-permute-start.41 = (bf16[64,768]{1,0:T(8,128)(2,1)}, bf16[64,768]{1,0:T(8,128)(2,1)S(1)}, u32[]{:S(2)}, u32[]{:S(2)}) collective-permute-start(bf16[64,768]{1,0:T(8,128)(2,1)} %get-tuple-element.80), channel_id=1, source_target_pairs={{0,1},{1,2},{2,3},{3,0},{4,5},{5,6},{6,7},{7,4},{8,9},{9,10},{10,1... | collective-permute-start | bytes 294920 | tf_op jit(solution)/shard_map/ppermute | solution.py:1080
  275.8 50.2 %collective-permute-start.42 = (bf16[64,768]{1,0:T(8,128)(2,1)}, bf16[64,768]{1,0:T(8,128)(2,1)S(1)}, u32[]{:S(2)}, u32[]{:S(2)}) collective-permute-start(bf16[64,768]{1,0:T(8,128)(2,1)} %get-tuple-element.80), channel_id=1, source_target_pairs={{0,2},{1,3},{2,0},{3,1},{4,6},{5,7},{6,4},{7,5},{8,10},{9,11},{10,... | collective-permute-start | bytes 294920 | tf_op jit(solution)/shard_map/ppermute | solution.py:1080
  324.0 14.3 %collective-permute-start.45 = (bf16[320,768]{1,0:T(8,128)(2,1)}, bf16[320,768]{1,0:T(8,128)(2,1)S(1)}, u32[]{:S(2)}, u32[]{:S(2)}) collective-permute-start(bf16[320,768]{1,0:T(8,128)(2,1)} %get-tuple-element.84), channel_id=1, source_target_pairs={{0,8},{4,12},{8,0},{12,4},{16,24},{20,28},{24,16},{28,20},{1,9},{5... | collective-permute-start | bytes 1474568 | tf_op jit(solution)/shard_map/ppermute | solution.py:942
  325.7 23.5 %collective-permute-start.46 = (bf16[320,768]{1,0:T(8,128)(2,1)}, bf16[320,768]{1,0:T(8,128)(2,1)S(1)}, u32[]{:S(2)}, u32[]{:S(2)}) collective-permute-start(bf16[320,768]{1,0:T(8,128)(2,1)} %get-tuple-element.85), channel_id=1, source_target_pairs={{0,16},{4,20},{8,24},{12,28},{16,0},{20,4},{24,8},{28,12},{1,17},{... | collective-permute-start | bytes 1474568 | tf_op jit(solution)/shard_map/ppermute | solution.py:942
  326.0 23.2 %collective-permute-start.47 = (bf16[320,768]{1,0:T(8,128)(2,1)}, bf16[320,768]{1,0:T(8,128)(2,1)S(1)}, u32[]{:S(2)}, u32[]{:S(2)}) collective-permute-start(bf16[320,768]{1,0:T(8,128)(2,1)} %get-tuple-element.86), channel_id=1, source_target_pairs={{0,24},{4,28},{8,16},{12,20},{16,8},{20,12},{24,0},{28,4},{1,25},{... | collective-permute-start | bytes 1474568 | tf_op jit(solution)/shard_map/ppermute | solution.py:942
  338.3 21.1 %collective-permute-start.43 = (bf16[64,768]{1,0:T(8,128)(2,1)}, bf16[64,768]{1,0:T(8,128)(2,1)}, u32[]{:S(2)}, u32[]{:S(2)}) collective-permute-start(bf16[64,768]{1,0:T(8,128)(2,1)} %get-tuple-element.80), channel_id=1, source_target_pairs={{0,3},{1,0},{2,1},{3,2},{4,7},{5,4},{6,5},{7,6},{8,11},{9,8},{10,9... | collective-permute-start | bytes 294920 | tf_op jit(solution)/shard_map/ppermute | solution.py:1080
  357.3 14.0 %collective-permute-start.48 = (bf16[80,768]{1,0:T(8,128)(2,1)}, bf16[80,768]{1,0:T(8,128)(2,1)S(1)}, u32[]{:S(2)}, u32[]{:S(2)}) collective-permute-start(bf16[80,768]{1,0:T(8,128)(2,1)} %get-tuple-element.154), channel_id=1, source_target_pairs={{0,1},{1,2},{2,3},{3,0},{4,5},{5,6},{6,7},{7,4},{8,9},{9,10},{10,1... | collective-permute-start | bytes 368648 | tf_op jit(solution)/shard_map/ppermute | solution.py:1080
  359.2 13.5 %collective-permute-start.49 = (bf16[80,768]{1,0:T(8,128)(2,1)}, bf16[80,768]{1,0:T(8,128)(2,1)}, u32[]{:S(2)}, u32[]{:S(2)}) collective-permute-start(bf16[80,768]{1,0:T(8,128)(2,1)} %get-tuple-element.153), channel_id=1, source_target_pairs={{0,2},{1,3},{2,0},{3,1},{4,6},{5,7},{6,4},{7,5},{8,10},{9,11},{10,... | collective-permute-start | bytes 368648 | tf_op jit(solution)/shard_map/ppermute | solution.py:1080
  359.3 13.8 %collective-permute-start.50 = (bf16[80,768]{1,0:T(8,128)(2,1)}, bf16[80,768]{1,0:T(8,128)(2,1)}, u32[]{:S(2)}, u32[]{:S(2)}) collective-permute-start(bf16[80,768]{1,0:T(8,128)(2,1)} %get-tuple-element.152), channel_id=1, source_target_pairs={{0,3},{1,0},{2,1},{3,2},{4,7},{5,4},{6,5},{7,6},{8,11},{9,8},{10,9... | collective-permute-start | bytes 368648 | tf_op jit(solution)/shard_map/ppermute | solution.py:1080
  369.6 26.4 %collective-permute-start.60 = (bf16[784,384]{1,0:T(8,128)(2,1)}, bf16[784,384]{1,0:T(8,128)(2,1)S(1)}, u32[]{:S(2)}, u32[]{:S(2)}) collective-permute-start(bf16[784,384]{1,0:T(8,128)(2,1)} %get-tuple-element.96), channel_id=1, source_target_pairs={{0,8},{4,12},{8,0},{12,4},{16,24},{20,28},{24,16},{28,20},{1,9},{5... | collective-permute-start | bytes 1806344 | tf_op jit(solution)/shard_map/ppermute | solution.py:942
  371.2 25.5 %collective-permute-start.61 = (bf16[784,384]{1,0:T(8,128)(2,1)}, bf16[784,384]{1,0:T(8,128)(2,1)S(1)}, u32[]{:S(2)}, u32[]{:S(2)}) collective-permute-start(bf16[784,384]{1,0:T(8,128)(2,1)} %get-tuple-element.97), channel_id=1, source_target_pairs={{0,16},{4,20},{8,24},{12,28},{16,0},{20,4},{24,8},{28,12},{1,17},{... | collective-permute-start | bytes 1806344 | tf_op jit(solution)/shard_map/ppermute | solution.py:942
  372.7 24.0 %collective-permute-start.62 = (bf16[784,384]{1,0:T(8,128)(2,1)}, bf16[784,384]{1,0:T(8,128)(2,1)}, u32[]{:S(2)}, u32[]{:S(2)}) collective-permute-start(bf16[784,384]{1,0:T(8,128)(2,1)} %get-tuple-element.98), channel_id=1, source_target_pairs={{0,24},{4,28},{8,16},{12,20},{16,8},{20,12},{24,0},{28,4},{1,25},{... | collective-permute-start | bytes 1806344 | tf_op jit(solution)/shard_map/ppermute | solution.py:942
  401.0 10.9 %collective-permute-start.63 = (bf16[784,384]{1,0:T(8,128)(2,1)}, bf16[784,384]{1,0:T(8,128)(2,1)S(1)}, u32[]{:S(2)}, u32[]{:S(2)}) collective-permute-start(bf16[784,384]{1,0:T(8,128)(2,1)} %sum_parts.7), channel_id=1, source_target_pairs={{0,1},{1,0},{2,3},{3,2},{4,5},{5,4},{6,7},{7,6},{8,9},{9,8},{10,11... | collective-permute-start | bytes 1806344 | tf_op jit(solution)/shard_map/ppermute | solution.py:1118
  418.2 25.0 %collective-permute-start.55 = (bf16[1280,384]{1,0:T(8,128)(2,1)}, bf16[1280,384]{1,0:T(8,128)(2,1)}, u32[]{:S(2)}, u32[]{:S(2)}) collective-permute-start(bf16[1280,384]{1,0:T(8,128)(2,1)} %get-tuple-element.90), channel_id=1, source_target_pairs={{0,8},{4,12},{8,0},{12,4},{16,24},{20,28},{24,16},{28,20},{1,9},{5... | collective-permute-start | bytes 2949128 | tf_op jit(solution)/shard_map/ppermute | solution.py:942
  418.9 40.0 %collective-permute-start.56 = (bf16[1280,384]{1,0:T(8,128)(2,1)}, bf16[1280,384]{1,0:T(8,128)(2,1)}, u32[]{:S(2)}, u32[]{:S(2)}) collective-permute-start(bf16[1280,384]{1,0:T(8,128)(2,1)} %get-tuple-element.91), channel_id=1, source_target_pairs={{0,16},{4,20},{8,24},{12,28},{16,0},{20,4},{24,8},{28,12},{1,17},{... | collective-permute-start | bytes 2949128 | tf_op jit(solution)/shard_map/ppermute | solution.py:942
  420.7 40.0 %collective-permute-start.57 = (bf16[1280,384]{1,0:T(8,128)(2,1)}, bf16[1280,384]{1,0:T(8,128)(2,1)}, u32[]{:S(2)}, u32[]{:S(2)}) collective-permute-start(bf16[1280,384]{1,0:T(8,128)(2,1)} %get-tuple-element.92), channel_id=1, source_target_pairs={{0,24},{4,28},{8,16},{12,20},{16,8},{20,12},{24,0},{28,4},{1,25},{... | collective-permute-start | bytes 2949128 | tf_op jit(solution)/shard_map/ppermute | solution.py:942
  464.6 18.5 %collective-permute-start.58 = (bf16[1280,384]{1,0:T(8,128)(2,1)}, bf16[1280,384]{1,0:T(8,128)(2,1)S(1)}, u32[]{:S(2)}, u32[]{:S(2)}) collective-permute-start(bf16[1280,384]{1,0:T(8,128)(2,1)} %sum_parts.6), channel_id=1, source_target_pairs={{0,1},{1,0},{2,3},{3,2},{4,5},{5,4},{6,7},{7,6},{8,9},{9,8},{10,11... | collective-permute-start | bytes 2949128 | tf_op jit(solution)/shard_map/ppermute | solution.py:1118
  (60 other events, 556.2 us)
